TPU v7x, 128 devices: a whole 4x4x4 slice. The times are simulated.
128 devices in a mesh: probe: 4 (over z_hi, core), sx: 4 (over x), sy: 8 (over y, z_lo).
Axes of the slice: x: 4, y: 4, z: 4 (z_hi: 2, z_lo: 2; z = z_hi * 2 + z_lo), core: 2. Of those that a mesh axis runs over, the one named last changes fastest.
Arguments:
- probes: float32 [8, 128, 256, 256], P('probe', 'sx', 'sy'), may hold values from -6 to 6
- velocity: float32 [3, 128, 256, 256], P(None, 'sx', 'sy'), may hold values from -0.15 to 0.15
- diffusivity: float32 [128, 256, 256], P('sx', 'sy'), may hold values from 0.02 to 0.15
- obs_weight: float32 [128, 256, 256], P('sx', 'sy'), may hold values from 0.05 to 1
Outputs:
- basis_fields: float32 [8, 128, 256, 256], P('probe', 'sx', 'sy')
- projected_hessian: float32 [8, 8], replicated
All inputs are finite; a program needn't handle non-finite values.
Results may differ from a plain program's by a relative error of at most 0.00013.
Values sent between devices are 32-bit elements; how exact they have to be, the bound alone decides.
A program may use at most 128 MiB of HBM per device.

v0:
```python
import jax
import jax.numpy as jnp
from jax import lax
from jax.sharding import PartitionSpec as P

STEPS = 4


def extended(value, sides, width):
    for axis, dim in sides:
        devices, length = (lax.axis_size(axis), value.shape[dim])
        up = [(i, (i + 1) % devices) for i in range(devices - 1)]
        down = [(j, i) for i, j in up]
        last = lax.slice_in_dim(value, length - width, length, axis=dim)
        leading = lax.slice_in_dim(value, 0, width, axis=dim)
        before = lax.ppermute(last, axis, up)
        after = lax.ppermute(leading, axis, down)
        value = jnp.concatenate([before, value, after], axis=dim)
    return value


def forward_step(state, coeffs):
    cc = coeffs[:, 1:-1, 1:-1, :]
    spread = cc[0]
    inner = state[:, 1:-1, 1:-1, :]
    padded = jnp.pad(inner, ((0, 0), (0, 0), (0, 0), (1, 1)))
    result = (1.0 - 6.0 * spread) * inner
    result = (
        result
        + (spread - 0.5 * cc[1]) * state[:, 2:, 1:-1, :]
        + (spread + 0.5 * cc[1]) * state[:, :-2, 1:-1, :]
    )
    result = (
        result
        + (spread - 0.5 * cc[2]) * state[:, 1:-1, 2:, :]
        + (spread + 0.5 * cc[2]) * state[:, 1:-1, :-2, :]
    )
    result = (
        result
        + (spread - 0.5 * cc[3]) * padded[..., 2:]
        + (spread + 0.5 * cc[3]) * padded[..., :-2]
    )
    return result


def adjoint_step(state, coeffs):
    spread = coeffs[0]
    plus_x = (spread - 0.5 * coeffs[1]) * state
    minus_x = (spread + 0.5 * coeffs[1]) * state
    plus_y = (spread - 0.5 * coeffs[2]) * state
    minus_y = (spread + 0.5 * coeffs[2]) * state
    cc = coeffs[:, 1:-1, 1:-1, :]
    inner = state[:, 1:-1, 1:-1, :]
    pad_plus = jnp.pad((cc[0] - 0.5 * cc[3]) * inner, ((0, 0), (0, 0), (0, 0), (1, 1)))
    pad_minus = jnp.pad((cc[0] + 0.5 * cc[3]) * inner, ((0, 0), (0, 0), (0, 0), (1, 1)))
    result = (1.0 - 6.0 * cc[0]) * inner
    result = result + plus_x[:, :-2, 1:-1, :] + minus_x[:, 2:, 1:-1, :]
    result = result + plus_y[:, 1:-1, :-2, :] + minus_y[:, 1:-1, 2:, :]
    result = result + pad_plus[..., :-2] + pad_minus[..., 2:]
    return result


def factor_inverse(gram, count):
    lower = jnp.linalg.cholesky(gram)
    return jax.scipy.linalg.solve_triangular(lower, jnp.eye(count, dtype=jnp.float32), lower=True)


def shards(probes, velocity, diffusivity, obs_weight):
    group = probes.shape[0]
    count = group * lax.axis_size("probe")
    ncells = (
        probes.shape[1]
        * probes.shape[2]
        * probes.shape[3]
        * lax.axis_size("sx")
        * lax.axis_size("sy")
    )
    coeffs = jnp.concatenate([diffusivity[None], velocity], axis=0)
    highest = lax.Precision.HIGHEST
    edge_coeffs = extended(coeffs, (("sx", 1), ("sy", 2)), 1)

    def hessian(field):
        state = field
        for step in range(STEPS):
            padded = extended(state, (("sx", 1), ("sy", 2)), 1)
            state = forward_step(padded, edge_coeffs)
        state = obs_weight * state
        for step in range(STEPS):
            padded = extended(state, (("sx", 1), ("sy", 2)), 1)
            state = adjoint_step(padded, edge_coeffs)
        return state

    images = hessian(probes)
    slabs = lax.all_to_all(images, "probe", split_axis=1, concat_axis=0, tiled=True)
    flat = slabs.reshape(count, -1)
    partial_gram = jnp.dot(flat, flat.T, precision=highest)
    gram = lax.psum(partial_gram, ("probe", "sx", "sy")) / ncells
    inverse = factor_inverse(gram, count)
    basis_slab = jnp.dot(inverse, flat, precision=highest)
    basis_fields = lax.all_to_all(
        basis_slab.reshape(slabs.shape), "probe", split_axis=0, concat_axis=1, tiled=True
    )
    second = hessian(basis_fields)
    second_slab = lax.all_to_all(second, "probe", split_axis=1, concat_axis=0, tiled=True).reshape(
        count, -1
    )
    partial_ritz = jnp.dot(basis_slab, second_slab.T, precision=highest)
    projected = lax.psum(partial_ritz, ("probe", "sx", "sy")) / ncells
    return (basis_fields, projected)


def solution(mesh):
    return jax.shard_map(
        shards,
        mesh=mesh,
        in_specs=(
            P("probe", "sx", "sy", None),
            P(None, "sx", "sy", None),
            P("sx", "sy", None),
            P("sx", "sy", None),
        ),
        out_specs=(P("probe", "sx", "sy", None), P()),
        check_vma=False,
    )
```

profile of v0, /device:TPU:1, one launch (start us, length us, event | category | flops | bytes accessed | tf_op | source)
XLA Modules:
  0.0 624.0 jit_solution(7994975373711091227)
XLA Ops:
  3.0 4.6 collective-permute-start.1
  12.0 4.4 collective-permute-start.3
  34.8 4.9 collective-permute-start.7
  54.7 4.9 collective-permute-start.18
  61.0 5.1 collective-permute-start.11
  82.7 4.7 collective-permute-start.15
  100.4 4.3 collective-permute-start.22
  106.3 4.7 collective-permute-done.23
  160.9 4.6 collective-permute-start.34
  175.1 49.0 %all_to_all.48 = f32[2,32,32,256]{3,2,0,1:T(8,128)S(1)} all-to-all(f32[2,32,32,256]{3,2,0,1:T(8,128)S(1)} %copy.72), channel_id=1, replica_groups=mesh['probe'=4,'sx'=4,'sy'=8] {'probe'}, dimensions={1} | all-to-all | bytes 4194304 | tf_op jit(solution)/shard_map/all_to_all | solution.py:94
  228.8 6.8 %fusion.176 = f32[8,8]{0,1:T(8,128)S(1)} fusion(f32[8,65536]{1,0:T(8,128)} %reshape.39), kind=kOutput, calls=%fused_computation.405 | convolution fusion | flops 50331648 | bytes 2097408 | tf_op jit(solution)/shard_map/dot_general | solution.py:96
  235.6 62.9 %psum.14 = f32[8,8]{0,1:T(8,128)S(1)} all-reduce(f32[8,8]{0,1:T(8,128)S(1)} %fusion.176), channel_id=1, replica_groups=mesh['probe'=4,'sx'=4,'sy'=8] {'probe','sx','sy'}, use_global_device_ids=true, to_apply=%region_0.1 | all-reduce | flops 64 | bytes 512 | tf_op jit(solution)/shard_map/psum | solution.py:97
  306.2 29.8 %all_to_all.49 = f32[8,8,32,256]{3,2,1,0:T(8,128)S(1)} all-to-all(f32[8,8,32,256]{3,2,1,0:T(8,128)S(1)} %copy.77), channel_id=1, replica_groups=mesh['probe'=4,'sx'=4,'sy'=8] {'probe'}, dimensions={0} | all-to-all | bytes 4194304 | tf_op jit(solution)/shard_map/all_to_all | solution.py:100
  363.8 4.3 collective-permute-start.43
  382.4 5.1 collective-permute-start.47
  401.0 5.1 collective-permute-start.51
  418.3 4.7 collective-permute-start.54
  424.7 5.1 collective-permute-done.55
  439.8 4.3 collective-permute-start.58
  484.1 4.4 collective-permute-done.67
  494.2 27.0 %all-to-all-start.2 = ((f32[2,32,32,256]{3,2,0,1:T(8,128)}), f32[2,32,32,256]{3,2,0,1:T(8,128)}, u32[]{:S(2)}, u32[]{:S(2)}) async-start(f32[2,32,32,256]{3,2,0,1:T(8,128)} %copy.79), calls=%async_computation.2 | async-start | bytes 4194304 | tf_op jit(solution)/shard_map/all_to_all | solution.py:104
  523.7 23.7 %all-to-all-done.2 = f32[2,32,32,256]{3,2,0,1:T(8,128)} async-done(((f32[2,32,32,256]{3,2,0,1:T(8,128)}), f32[2,32,32,256]{3,2,0,1:T(8,128)}, u32[]{:S(2)}, u32[]{:S(2)}) %all-to-all-start.2) | async-done | bytes 2097184 | tf_op jit(solution)/shard_map/all_to_all | solution.py:104
  554.1 6.2 fusion.178
  560.3 62.7 %psum.15 = f32[8,8]{0,1:T(8,128)S(1)} all-reduce(f32[8,8]{0,1:T(8,128)S(1)} %fusion.178), channel_id=1, replica_groups=mesh['probe'=4,'sx'=4,'sy'=8] {'probe','sx','sy'}, use_global_device_ids=true, to_apply=%region_3.4 | all-reduce | flops 64 | bytes 512 | tf_op jit(solution)/shard_map/psum | solution.py:108
  (286 shorter events, 277.9 us)
Async XLA Ops:
  1.6 8.9 %collective-permute-start = (f32[2,1,32,256]{3,1,2,0:T(1,128)S(1)}, f32[2,1,32,256]{3,1,2,0:T(1,128)S(1)}, u32[]{:S(2)}, u32[]{:S(2)}) collective-permute-start(f32[2,1,32,256]{3,1,2,0:T(1,128)S(1)} %copy.53), channel_id=1, source_target_pairs={{8,0},{16,8},{24,16},{9,1},{17,9},{25,17},{10,2},{18,10},{26,18},{... | collective-permute-start | bytes 196616 | tf_op jit(solution)/shard_map/ppermute | solution.py:17
  3.0 7.6 %collective-permute-start.1 = (f32[2,1,32,256]{3,1,2,0:T(1,128)S(1)}, f32[2,1,32,256]{3,1,2,0:T(1,128)S(1)}, u32[]{:S(2)}, u32[]{:S(2)}) collective-permute-start(f32[2,1,32,256]{3,1,2,0:T(1,128)S(1)} %copy.56), channel_id=1, source_target_pairs={{0,8},{8,16},{16,24},{1,9},{9,17},{17,25},{2,10},{10,18},{18,26},{... | collective-permute-start | bytes 196616 | tf_op jit(solution)/shard_map/ppermute | solution.py:16
  10.6 11.3 %collective-permute-start.2 = (f32[2,34,1,256]{3,1,2,0:T(8,128)S(1)}, f32[2,34,1,256]{3,1,2,0:T(8,128)S(1)}, u32[]{:S(2)}, u32[]{:S(2)}) collective-permute-start(f32[2,34,1,256]{3,1,2,0:T(8,128)S(1)} %get-tuple-element.71), channel_id=1, source_target_pairs={{1,0},{2,1},{3,2},{4,3},{5,4},{6,5},{7,6},{9,8},{10,9},{11,10},{12... | collective-permute-start | bytes 208904 | tf_op jit(solution)/shard_map/ppermute | solution.py:17
  12.0 9.9 %collective-permute-start.3 = (f32[2,34,1,256]{3,1,2,0:T(8,128)S(1)}, f32[2,34,1,256]{3,1,2,0:T(8,128)S(1)}, u32[]{:S(2)}, u32[]{:S(2)}) collective-permute-start(f32[2,34,1,256]{3,1,2,0:T(8,128)S(1)} %get-tuple-element.72), channel_id=1, source_target_pairs={{0,1},{1,2},{2,3},{3,4},{4,5},{5,6},{6,7},{8,9},{9,10},{10,11},{11... | collective-permute-start | bytes 208904 | tf_op jit(solution)/shard_map/ppermute | solution.py:16
  33.5 10.7 %collective-permute-start.6 = (f32[2,34,1,256]{3,1,2,0:T(8,128)S(1)}, f32[2,34,1,256]{3,1,2,0:T(8,128)S(1)}, u32[]{:S(2)}, u32[]{:S(2)}) collective-permute-start(f32[2,34,1,256]{3,1,2,0:T(8,128)S(1)} %get-tuple-element.69), channel_id=1, source_target_pairs={{1,0},{2,1},{3,2},{4,3},{5,4},{6,5},{7,6},{9,8},{10,9},{11,10},{12... | collective-permute-start | bytes 208904 | tf_op jit(solution)/shard_map/ppermute | solution.py:17
  34.8 9.4 %collective-permute-start.7 = (f32[2,34,1,256]{3,1,2,0:T(8,128)S(1)}, f32[2,34,1,256]{3,1,2,0:T(8,128)S(1)}, u32[]{:S(2)}, u32[]{:S(2)}) collective-permute-start(f32[2,34,1,256]{3,1,2,0:T(8,128)S(1)} %get-tuple-element.70), channel_id=1, source_target_pairs={{0,1},{1,2},{2,3},{3,4},{4,5},{5,6},{6,7},{8,9},{9,10},{10,11},{11... | collective-permute-start | bytes 208904 | tf_op jit(solution)/shard_map/ppermute | solution.py:16
  39.8 13.2 %collective-permute-start.16 = (f32[4,1,32,256]{3,2,1,0:T(8,128)S(1)}, f32[4,1,32,256]{3,2,1,0:T(8,128)S(1)}, u32[]{:S(2)}, u32[]{:S(2)}) collective-permute-start(f32[4,1,32,256]{3,2,1,0:T(8,128)S(1)} %get-tuple-element.33), channel_id=1, source_target_pairs={{0,8},{8,16},{16,24},{1,9},{9,17},{17,25},{2,10},{10,18},{18,26},{... | collective-permute-start | bytes 393224 | tf_op jit(solution)/shard_map/ppermute | solution.py:16
  42.9 10.1 %collective-permute-start.17 = (f32[4,1,32,256]{3,2,1,0:T(8,128)S(1)}, f32[4,1,32,256]{3,2,1,0:T(8,128)S(1)}, u32[]{:S(2)}, u32[]{:S(2)}) collective-permute-start(f32[4,1,32,256]{3,2,1,0:T(8,128)S(1)} %get-tuple-element.34), channel_id=1, source_target_pairs={{8,0},{16,8},{24,16},{9,1},{17,9},{25,17},{10,2},{18,10},{26,18},{... | collective-permute-start | bytes 393224 | tf_op jit(solution)/shard_map/ppermute | solution.py:17
  47.7 11.9 %collective-permute-start.9 = (f32[2,1,32,256]{3,1,2,0:T(1,128)S(1)}, f32[2,1,32,256]{3,1,2,0:T(1,128)S(1)}, u32[]{:S(2)}, u32[]{:S(2)}) collective-permute-start(f32[2,1,32,256]{3,1,2,0:T(1,128)S(1)} %get-tuple-element.99), channel_id=1, source_target_pairs={{0,8},{8,16},{16,24},{1,9},{9,17},{17,25},{2,10},{10,18},{18,26},{... | collective-permute-start | bytes 196616 | tf_op jit(solution)/shard_map/ppermute | solution.py:16
  51.7 7.9 %collective-permute-start.8 = (f32[2,1,32,256]{3,1,2,0:T(1,128)S(1)}, f32[2,1,32,256]{3,1,2,0:T(1,128)S(1)}, u32[]{:S(2)}, u32[]{:S(2)}) collective-permute-start(f32[2,1,32,256]{3,1,2,0:T(1,128)S(1)} %get-tuple-element.100), channel_id=1, source_target_pairs={{8,0},{16,8},{24,16},{9,1},{17,9},{25,17},{10,2},{18,10},{26,18},{... | collective-permute-start | bytes 196616 | tf_op jit(solution)/shard_map/ppermute | solution.py:17
  53.3 13.4 %collective-permute-start.19 = (f32[4,34,1,256]{3,1,2,0:T(8,128)S(1)}, f32[4,34,1,256]{3,1,2,0:T(8,128)S(1)}, u32[]{:S(2)}, u32[]{:S(2)}) collective-permute-start(f32[4,34,1,256]{3,1,2,0:T(8,128)S(1)} %copy.65), channel_id=1, source_target_pairs={{1,0},{2,1},{3,2},{4,3},{5,4},{6,5},{7,6},{9,8},{10,9},{11,10},{12... | collective-permute-start | bytes 417800 | tf_op jit(solution)/shard_map/ppermute | solution.py:17
  54.7 12.2 %collective-permute-start.18 = (f32[4,34,1,256]{3,1,2,0:T(8,128)S(1)}, f32[4,34,1,256]{3,1,2,0:T(8,128)S(1)}, u32[]{:S(2)}, u32[]{:S(2)}) collective-permute-start(f32[4,34,1,256]{3,1,2,0:T(8,128)S(1)} %copy.64), channel_id=1, source_target_pairs={{0,1},{1,2},{2,3},{3,4},{4,5},{5,6},{6,7},{8,9},{9,10},{10,11},{11... | collective-permute-start | bytes 417800 | tf_op jit(solution)/shard_map/ppermute | solution.py:16
  59.7 7.4 %collective-permute-start.10 = (f32[2,34,1,256]{3,1,2,0:T(8,128)S(1)}, f32[2,34,1,256]{3,1,2,0:T(8,128)S(1)}, u32[]{:S(2)}, u32[]{:S(2)}) collective-permute-start(f32[2,34,1,256]{3,1,2,0:T(8,128)S(1)} %get-tuple-element.67), channel_id=1, source_target_pairs={{1,0},{2,1},{3,2},{4,3},{5,4},{6,5},{7,6},{9,8},{10,9},{11,10},{12... | collective-permute-start | bytes 208904 | tf_op jit(solution)/shard_map/ppermute | solution.py:17
  61.0 7.7 %collective-permute-start.11 = (f32[2,34,1,256]{3,1,2,0:T(8,128)S(1)}, f32[2,34,1,256]{3,1,2,0:T(8,128)S(1)}, u32[]{:S(2)}, u32[]{:S(2)}) collective-permute-start(f32[2,34,1,256]{3,1,2,0:T(8,128)S(1)} %get-tuple-element.68), channel_id=1, source_target_pairs={{0,1},{1,2},{2,3},{3,4},{4,5},{5,6},{6,7},{8,9},{9,10},{10,11},{11... | collective-permute-start | bytes 208904 | tf_op jit(solution)/shard_map/ppermute | solution.py:16
  81.4 7.6 %collective-permute-start.14 = (f32[2,34,1,256]{3,1,2,0:T(8,128)S(1)}, f32[2,34,1,256]{3,1,2,0:T(8,128)S(1)}, u32[]{:S(2)}, u32[]{:S(2)}) collective-permute-start(f32[2,34,1,256]{3,1,2,0:T(8,128)S(1)} %get-tuple-element.65), channel_id=1, source_target_pairs={{1,0},{2,1},{3,2},{4,3},{5,4},{6,5},{7,6},{9,8},{10,9},{11,10},{12... | collective-permute-start | bytes 208904 | tf_op jit(solution)/shard_map/ppermute | solution.py:17
  92.5 7.8 %collective-permute-start.20 = (f32[2,1,32,256]{3,1,2,0:T(1,128)S(1)}, f32[2,1,32,256]{3,1,2,0:T(1,128)S(1)}, u32[]{:S(2)}, u32[]{:S(2)}) collective-permute-start(f32[2,1,32,256]{3,1,2,0:T(1,128)S(1)} %get-tuple-element.95), channel_id=1, source_target_pairs={{0,8},{8,16},{16,24},{1,9},{9,17},{17,25},{2,10},{10,18},{18,26},{... | collective-permute-start | bytes 196616 | tf_op jit(solution)/shard_map/ppermute | solution.py:16
  160.9 6.4 %collective-permute-start.34 = (f32[2,34,1,256]{3,1,2,0:T(8,128)S(1)}, f32[2,34,1,256]{3,1,2,0:T(8,128)S(1)}, u32[]{:S(2)}, u32[]{:S(2)}) collective-permute-start(f32[2,34,1,256]{3,1,2,0:T(8,128)S(1)} %get-tuple-element.57), channel_id=1, source_target_pairs={{0,1},{1,2},{2,3},{3,4},{4,5},{5,6},{6,7},{8,9},{9,10},{10,11},{11... | collective-permute-start | bytes 208904 | tf_op jit(solution)/shard_map/ppermute | solution.py:16
  381.1 6.6 %collective-permute-start.46 = (f32[2,34,1,256]{3,1,2,0:T(8,128)S(1)}, f32[2,34,1,256]{3,1,2,0:T(8,128)S(1)}, u32[]{:S(2)}, u32[]{:S(2)}) collective-permute-start(f32[2,34,1,256]{3,1,2,0:T(8,128)S(1)} %get-tuple-element.51), channel_id=1, source_target_pairs={{1,0},{2,1},{3,2},{4,3},{5,4},{6,5},{7,6},{9,8},{10,9},{11,10},{12... | collective-permute-start | bytes 208904 | tf_op jit(solution)/shard_map/ppermute | solution.py:17
  382.4 6.7 %collective-permute-start.47 = (f32[2,34,1,256]{3,1,2,0:T(8,128)S(1)}, f32[2,34,1,256]{3,1,2,0:T(8,128)S(1)}, u32[]{:S(2)}, u32[]{:S(2)}) collective-permute-start(f32[2,34,1,256]{3,1,2,0:T(8,128)S(1)} %get-tuple-element.52), channel_id=1, source_target_pairs={{0,1},{1,2},{2,3},{3,4},{4,5},{5,6},{6,7},{8,9},{9,10},{10,11},{11... | collective-permute-start | bytes 208904 | tf_op jit(solution)/shard_map/ppermute | solution.py:16
  399.7 6.5 %collective-permute-start.50 = (f32[2,34,1,256]{3,1,2,0:T(8,128)S(1)}, f32[2,34,1,256]{3,1,2,0:T(8,128)S(1)}, u32[]{:S(2)}, u32[]{:S(2)}) collective-permute-start(f32[2,34,1,256]{3,1,2,0:T(8,128)S(1)} %get-tuple-element.49), channel_id=1, source_target_pairs={{1,0},{2,1},{3,2},{4,3},{5,4},{6,5},{7,6},{9,8},{10,9},{11,10},{12... | collective-permute-start | bytes 208904 | tf_op jit(solution)/shard_map/ppermute | solution.py:17
  401.0 6.7 %collective-permute-start.51 = (f32[2,34,1,256]{3,1,2,0:T(8,128)S(1)}, f32[2,34,1,256]{3,1,2,0:T(8,128)S(1)}, u32[]{:S(2)}, u32[]{:S(2)}) collective-permute-start(f32[2,34,1,256]{3,1,2,0:T(8,128)S(1)} %get-tuple-element.50), channel_id=1, source_target_pairs={{0,1},{1,2},{2,3},{3,4},{4,5},{5,6},{6,7},{8,9},{9,10},{10,11},{11... | collective-permute-start | bytes 208904 | tf_op jit(solution)/shard_map/ppermute | solution.py:16
  418.3 6.4 %collective-permute-start.54 = (f32[2,34,1,256]{3,1,2,0:T(8,128)S(1)}, f32[2,34,1,256]{3,1,2,0:T(8,128)S(1)}, u32[]{:S(2)}, u32[]{:S(2)}) collective-permute-start(f32[2,34,1,256]{3,1,2,0:T(8,128)S(1)} %get-tuple-element.47), channel_id=1, source_target_pairs={{0,1},{1,2},{2,3},{3,4},{4,5},{5,6},{6,7},{8,9},{9,10},{10,11},{11... | collective-permute-start | bytes 208904 | tf_op jit(solution)/shard_map/ppermute | solution.py:16
  423.0 6.8 %collective-permute-start.55 = (f32[2,34,1,256]{3,1,2,0:T(8,128)S(1)}, f32[2,34,1,256]{3,1,2,0:T(8,128)S(1)}, u32[]{:S(2)}, u32[]{:S(2)}) collective-permute-start(f32[2,34,1,256]{3,1,2,0:T(8,128)S(1)} %get-tuple-element.48), channel_id=1, source_target_pairs={{1,0},{2,1},{3,2},{4,3},{5,4},{6,5},{7,6},{9,8},{10,9},{11,10},{12... | collective-permute-start | bytes 208904 | tf_op jit(solution)/shard_map/ppermute | solution.py:17
  494.2 53.3 %all-to-all-start.2 = ((f32[2,32,32,256]{3,2,0,1:T(8,128)}), f32[2,32,32,256]{3,2,0,1:T(8,128)}, u32[]{:S(2)}, u32[]{:S(2)}) async-start(f32[2,32,32,256]{3,2,0,1:T(8,128)} %copy.79), calls=%async_computation.2 | async-start | bytes 4194304 | tf_op jit(solution)/shard_map/all_to_all | solution.py:104
  (71 other events, 986.8 us)
where the time goes:
time: 634 us; the launch traced here: 624 us
  blocking collectives  204 us (32%)
  starting transfers between devices  193 us (30%)
  waiting for transfers between devices  111 us (18%)
  other arithmetic  60.5 us (10%)
  local copies, waits for them, and re-layouts  35.1 us (6%)
  matrix products  16.6 us (3%)
    ppermute x34, starting transfers between devices, extended(): before = lax.ppermute(last, axis, up)  122 us
    ppermute x34, waiting for transfers between devices, extended(): after = lax.ppermute(leading, axis, down)  78.5 us
    psum x1, blocking collectives, shards(): gram = lax.psum(partial_gram, ('probe', 'sx', 'sy')) / ncells  62.9 us
    psum x1, blocking collectives, shards(): projected = lax.psum(partial_ritz, ('probe', 'sx', 'sy')) / ncells  62.7 us
    all_to_all x1, blocking collectives, shards(): lax.all_to_all(images, 'probe', split_axis=1, concat_axis=0, tiled=True)  49 us
    ppermute x34, starting transfers between devices, extended(): after = lax.ppermute(leading, axis, down)  44.6 us
    all_to_all x1, blocking collectives, shards(): lax.all_to_all(basis_slab.reshape(slabs.shape), 'probe', split_axis=0, co...  29.8 us
    all_to_all x1, starting transfers between devices, shards(): lax.all_to_all(second, 'probe', split_axis=1, concat_axis=0, tiled=True)  27 us
  transfers between devices with their start and end apart: 69, of which 30 were waited for; matrix products, arithmetic and copies ran while one was open for 4% of the time, Pallas kernels for 0%

commit v1 on v0

--- a/solution.py
+++ b/solution.py
@@ -79,33 +79,35 @@
     highest = lax.Precision.HIGHEST
     edge_coeffs = extended(coeffs, (("sx", 1), ("sy", 2)), 1)
 
-    def hessian(field):
-        state = field
+    def forward(state):
         for step in range(STEPS):
             padded = extended(state, (("sx", 1), ("sy", 2)), 1)
             state = forward_step(padded, edge_coeffs)
-        state = obs_weight * state
-        for step in range(STEPS):
-            padded = extended(state, (("sx", 1), ("sy", 2)), 1)
-            state = adjoint_step(padded, edge_coeffs)
         return state
 
-    images = hessian(probes)
-    slabs = lax.all_to_all(images, "probe", split_axis=1, concat_axis=0, tiled=True)
-    flat = slabs.reshape(count, -1)
+    state = obs_weight * forward(probes)
+    for step in range(STEPS):
+        padded = extended(state, (("sx", 1), ("sy", 2)), 1)
+        state = adjoint_step(padded, edge_coeffs)
+    images = state
+    again = forward(images)
+    root = jnp.sqrt(obs_weight) * again
+    both = jnp.stack([images, root], axis=1)
+    slabs = lax.all_to_all(both, "probe", split_axis=2, concat_axis=0, tiled=True)
+    flat = slabs[:, 0].reshape(count, -1)
+    flat_root = slabs[:, 1].reshape(count, -1)
     partial_gram = jnp.dot(flat, flat.T, precision=highest)
-    gram = lax.psum(partial_gram, ("probe", "sx", "sy")) / ncells
+    partial_cross = jnp.dot(flat_root, flat_root.T, precision=highest)
+    sums = lax.psum(jnp.stack([partial_gram, partial_cross]), ("probe", "sx", "sy")) / ncells
+    gram, cross = sums[0], sums[1]
     inverse = factor_inverse(gram, count)
     basis_slab = jnp.dot(inverse, flat, precision=highest)
     basis_fields = lax.all_to_all(
-        basis_slab.reshape(slabs.shape), "probe", split_axis=0, concat_axis=1, tiled=True
+        basis_slab.reshape(slabs[:, 0].shape), "probe", split_axis=0, concat_axis=1, tiled=True
     )
-    second = hessian(basis_fields)
-    second_slab = lax.all_to_all(second, "probe", split_axis=1, concat_axis=0, tiled=True).reshape(
-        count, -1
+    projected = jnp.dot(
+        jnp.dot(inverse, cross, precision=highest), inverse.T, precision=highest
     )
-    partial_ritz = jnp.dot(basis_slab, second_slab.T, precision=highest)
-    projected = lax.psum(partial_ritz, ("probe", "sx", "sy")) / ncells
     return (basis_fields, projected)
 
 

time: 634 us -> 481 us (0.76)
  blocking collectives: 204 us -> 152 us
  starting transfers between devices: 193 us -> 147 us
  waiting for transfers between devices: 111 us -> 66.8 us
  other arithmetic: 60.5 us -> 53 us
    ppermute x34 -> x26, waiting for transfers between devices: 78.5 us -> 24.1 us  [extended(): after = lax.ppermute(leading, axis, down)]
    psum x2 -> x1, blocking collectives: 126 us -> 72.6 us  [shards(): lax.psum(jnp.stack([partial_gram, partial_cross]), ('probe', 'sx', 'sy'))]
    all_to_all x1, starting transfers between devices: 27 us -> 4.14 us  [shards(): lax.all_to_all(basis_slab.reshape(slabs[:, 0].shape), 'probe', split_axis...]
    ppermute x34 -> x26, starting transfers between devices: 122 us -> 109 us  [extended(): before = lax.ppermute(last, axis, up)]
    ppermute x34 -> x26, starting transfers between devices: 44.6 us -> 34.3 us  [extended(): after = lax.ppermute(leading, axis, down)]
    ppermute x34 -> x26, waiting for transfers between devices: 9.22 us -> 17.3 us  [extended(): before = lax.ppermute(last, axis, up)]
    mul x8 -> x4, other arithmetic: 22.5 us -> 15 us  [adjoint_step(): (cc[0] + 0.5 * cc[3]) * inner]
    reshape x3 -> x0, local copies, waits for them, and re-layouts: 7.38 us -> none  [the longest x1 3.44 us: shards(): lax.all_to_all(second, 'probe', split_axis=1, concat_axis=0, tiled=True)]
  transfers between devices with their start and end apart: 69 -> 53, of which waited for: 30 -> 21; matrix products, arithmetic and copies ran while one was open for 4% -> 5% of each run, Pallas kernels for 0% -> 0%
where the time goes in v1:
time: 481 us; the launch traced here: 472 us
  blocking collectives  152 us (32%)
  starting transfers between devices  147 us (31%)
  waiting for transfers between devices  66.8 us (14%)
  other arithmetic  53 us (11%)
  local copies, waits for them, and re-layouts  31.4 us (7%)
  matrix products  18.7 us (4%)
    ppermute x26, starting transfers between devices, extended(): before = lax.ppermute(last, axis, up)  109 us
    all_to_all x1, blocking collectives, shards(): lax.all_to_all(both, 'probe', split_axis=2, concat_axis=0, tiled=True)  79.6 us
    psum x1, blocking collectives, shards(): lax.psum(jnp.stack([partial_gram, partial_cross]), ('probe', 'sx', 'sy'))  72.6 us
    ppermute x26, starting transfers between devices, extended(): after = lax.ppermute(leading, axis, down)  34.3 us
    all_to_all x1, waiting for transfers between devices, shards(): lax.all_to_all(basis_slab.reshape(slabs[:, 0].shape), 'probe', split_axis...  25.3 us
    ppermute x26, waiting for transfers between devices, extended(): after = lax.ppermute(leading, axis, down)  24.1 us
    add x6, other arithmetic, forward_step(): result + (spread - 0.5 * cc[3]) * padded[..., 2:]  20.5 us
    ppermute x26, waiting for transfers between devices, extended(): before = lax.ppermute(last, axis, up)  17.3 us
  transfers between devices with their start and end apart: 53, of which 21 were waited for; matrix products, arithmetic and copies ran while one was open for 5% of the time, Pallas kernels for 0%

profile of v1, /device:TPU:1, one launch (start us, length us, event | category | flops | bytes accessed | tf_op | source)
XLA Modules:
  0.0 471.6 jit_solution(13638757533432052887)
XLA Ops:
  3.0 4.6 collective-permute-start.1
  12.0 4.4 collective-permute-start.3
  33.3 4.9 %collective-permute-start.7 = (f32[2,34,1,256]{3,1,2,0:T(8,128)S(1)}, f32[2,34,1,256]{3,1,2,0:T(8,128)S(1)}, u32[]{:S(2)}, u32[]{:S(2)}) collective-permute-start(f32[2,34,1,256]{3,1,2,0:T(8,128)S(1)} %get-tuple-element.46), channel_id=1, source_target_pairs={{0,1},{1,2},{2,3},{3,4},{4,5},{5,6},{6,7},{8,9},{9,10},{10,11},{11... | collective-permute-start | bytes 208904 | tf_op jit(solution)/shard_map/ppermute | solution.py:16
  48.4 4.6 collective-permute-start.9
  53.3 4.4 collective-permute-start.18
  60.4 4.8 %collective-permute-start.11 = (f32[2,34,1,256]{3,1,2,0:T(8,128)S(1)}, f32[2,34,1,256]{3,1,2,0:T(8,128)S(1)}, u32[]{:S(2)}, u32[]{:S(2)}) collective-permute-start(f32[2,34,1,256]{3,1,2,0:T(8,128)S(1)} %get-tuple-element.44), channel_id=1, source_target_pairs={{0,1},{1,2},{2,3},{3,4},{4,5},{5,6},{6,7},{8,9},{9,10},{10,11},{11... | collective-permute-start | bytes 208904 | tf_op jit(solution)/shard_map/ppermute | solution.py:16
  73.1 4.3 collective-permute-start.13
  80.0 4.4 collective-permute-start.15
  98.3 4.3 collective-permute-start.22
  122.1 4.3 collective-permute-start.26
  165.1 4.3 collective-permute-start.34
  203.5 4.4 collective-permute-start.43
  215.3 4.4 collective-permute-start.45
  222.4 4.4 collective-permute-start.47
  233.2 4.6 collective-permute-start.49
  240.4 5.3 %collective-permute-start.51 = (f32[2,34,1,256]{3,1,2,0:T(8,128)S(1)}, f32[2,34,1,256]{3,1,2,0:T(8,128)S(1)}, u32[]{:S(2)}, u32[]{:S(2)}) collective-permute-start(f32[2,34,1,256]{3,1,2,0:T(8,128)S(1)} %get-tuple-element.26), channel_id=1, source_target_pairs={{0,1},{1,2},{2,3},{3,4},{4,5},{5,6},{6,7},{8,9},{9,10},{10,11},{11... | collective-permute-start | bytes 208904 | tf_op jit(solution)/shard_map/ppermute | solution.py:16
  253.3 79.6 %all_to_all.36 = f32[2,2,32,32,256]{4,3,0,1,2:T(8,128)S(1)} all-to-all(f32[2,2,32,32,256]{4,3,0,1,2:T(8,128)S(1)} %copy.58), channel_id=1, replica_groups=mesh['probe'=4,'sx'=4,'sy'=8] {'probe'}, dimensions={2} | all-to-all | bytes 8388608 | tf_op jit(solution)/shard_map/all_to_all | solution.py:96
  333.0 5.2 %copy.72 = f32[2,2,4,8,32,256]{5,0,2,4,3,1:T(2,128)} copy(f32[2,2,4,8,32,256]{5,4,0,1,3,2:T(8,128)S(1)} %bitcast.90) | data formatting | bytes 8388608 | tf_op jit(solution)/shard_map/all_to_all | solution.py:96
  338.2 6.1 %all_to_all.29 = f32[8,2,8,32,256]{4,0,3,2,1:T(8,128)} reshape(f32[4,2,2,8,32,256]{5,1,0,4,3,2:T(2,128)} %bitcast.91) | data formatting | bytes 8388608 | tf_op jit(solution)/shard_map/all_to_all | solution.py:96
  344.4 7.1 %fusion.131 = f32[1,8,8]{2,1,0:T(8,128)S(1)} fusion(f32[8,2,8,32,256]{4,0,3,2,1:T(8,128)} %all_to_all.29), kind=kOutput, calls=%fused_computation.253 | convolution fusion | flops 50331648 | bytes 2097408 | tf_op jit(solution)/shard_map/dot_general | solution.py:99
  351.5 7.1 %fusion.134 = f32[1,8,8]{2,1,0:T(8,128)S(1)} fusion(f32[8,2,8,32,256]{4,0,3,2,1:T(8,128)} %all_to_all.29), kind=kOutput, calls=%fused_computation.254 | convolution fusion | flops 50331648 | bytes 2097408 | tf_op jit(solution)/shard_map/dot_general | solution.py:100
  358.6 72.6 %psum.7 = f32[2,8,8]{2,1,0:T(8,128)S(1)} all-reduce(f32[2,8,8]{2,1,0:T(8,128)S(1)} %pad_maximum_fusion.117), channel_id=1, replica_groups=mesh['probe'=4,'sx'=4,'sy'=8] {'probe','sx','sy'}, use_global_device_ids=true, to_apply=%region_0.1 | all-reduce | flops 128 | bytes 1024 | tf_op jit(solution)/shard_map/psum | solution.py:101
  439.6 4.1 all-to-all-start.1
  444.6 25.3 %all-to-all-done.1 = f32[8,8,32,256]{3,2,1,0:T(8,128)S(1)} async-done(((f32[8,8,32,256]{3,2,1,0:T(8,128)}), f32[8,8,32,256]{3,2,1,0:T(8,128)S(1)}, u32[]{:S(2)}, u32[]{:S(2)}) %all-to-all-start.1) | async-done | bytes 2097184 | tf_op jit(solution)/shard_map/all_to_all | solution.py:105
  (191 shorter events, 189.7 us)
Async XLA Ops:
  1.6 8.9 %collective-permute-start = (f32[2,1,32,256]{3,1,2,0:T(1,128)S(1)}, f32[2,1,32,256]{3,1,2,0:T(1,128)S(1)}, u32[]{:S(2)}, u32[]{:S(2)}) collective-permute-start(f32[2,1,32,256]{3,1,2,0:T(1,128)S(1)} %copy.38), channel_id=1, source_target_pairs={{8,0},{16,8},{24,16},{9,1},{17,9},{25,17},{10,2},{18,10},{26,18},{... | collective-permute-start | bytes 196616 | tf_op jit(solution)/shard_map/ppermute | solution.py:17
  3.0 7.6 %collective-permute-start.1 = (f32[2,1,32,256]{3,1,2,0:T(1,128)S(1)}, f32[2,1,32,256]{3,1,2,0:T(1,128)S(1)}, u32[]{:S(2)}, u32[]{:S(2)}) collective-permute-start(f32[2,1,32,256]{3,1,2,0:T(1,128)S(1)} %copy.41), channel_id=1, source_target_pairs={{0,8},{8,16},{16,24},{1,9},{9,17},{17,25},{2,10},{10,18},{18,26},{... | collective-permute-start | bytes 196616 | tf_op jit(solution)/shard_map/ppermute | solution.py:16
  10.6 11.2 %collective-permute-start.2 = (f32[2,34,1,256]{3,1,2,0:T(8,128)S(1)}, f32[2,34,1,256]{3,1,2,0:T(8,128)S(1)}, u32[]{:S(2)}, u32[]{:S(2)}) collective-permute-start(f32[2,34,1,256]{3,1,2,0:T(8,128)S(1)} %get-tuple-element.47), channel_id=1, source_target_pairs={{1,0},{2,1},{3,2},{4,3},{5,4},{6,5},{7,6},{9,8},{10,9},{11,10},{12... | collective-permute-start | bytes 208904 | tf_op jit(solution)/shard_map/ppermute | solution.py:17
  12.0 9.8 %collective-permute-start.3 = (f32[2,34,1,256]{3,1,2,0:T(8,128)S(1)}, f32[2,34,1,256]{3,1,2,0:T(8,128)S(1)}, u32[]{:S(2)}, u32[]{:S(2)}) collective-permute-start(f32[2,34,1,256]{3,1,2,0:T(8,128)S(1)} %get-tuple-element.48), channel_id=1, source_target_pairs={{0,1},{1,2},{2,3},{3,4},{4,5},{5,6},{6,7},{8,9},{9,10},{10,11},{11... | collective-permute-start | bytes 208904 | tf_op jit(solution)/shard_map/ppermute | solution.py:16
  32.0 11.5 %collective-permute-start.6 = (f32[2,34,1,256]{3,1,2,0:T(8,128)S(1)}, f32[2,34,1,256]{3,1,2,0:T(8,128)S(1)}, u32[]{:S(2)}, u32[]{:S(2)}) collective-permute-start(f32[2,34,1,256]{3,1,2,0:T(8,128)S(1)} %get-tuple-element.45), channel_id=1, source_target_pairs={{1,0},{2,1},{3,2},{4,3},{5,4},{6,5},{7,6},{9,8},{10,9},{11,10},{12... | collective-permute-start | bytes 208904 | tf_op jit(solution)/shard_map/ppermute | solution.py:17
  33.3 10.2 %collective-permute-start.7 = (f32[2,34,1,256]{3,1,2,0:T(8,128)S(1)}, f32[2,34,1,256]{3,1,2,0:T(8,128)S(1)}, u32[]{:S(2)}, u32[]{:S(2)}) collective-permute-start(f32[2,34,1,256]{3,1,2,0:T(8,128)S(1)} %get-tuple-element.46), channel_id=1, source_target_pairs={{0,1},{1,2},{2,3},{3,4},{4,5},{5,6},{6,7},{8,9},{9,10},{10,11},{11... | collective-permute-start | bytes 208904 | tf_op jit(solution)/shard_map/ppermute | solution.py:16
  38.3 14.8 %collective-permute-start.16 = (f32[4,1,32,256]{3,2,1,0:T(8,128)S(1)}, f32[4,1,32,256]{3,2,1,0:T(8,128)S(1)}, u32[]{:S(2)}, u32[]{:S(2)}) collective-permute-start(f32[4,1,32,256]{3,2,1,0:T(8,128)S(1)} %get-tuple-element.17), channel_id=1, source_target_pairs={{0,8},{8,16},{16,24},{1,9},{9,17},{17,25},{2,10},{10,18},{18,26},{... | collective-permute-start | bytes 393224 | tf_op jit(solution)/shard_map/ppermute | solution.py:16
  42.3 10.8 %collective-permute-start.17 = (f32[4,1,32,256]{3,2,1,0:T(8,128)S(1)}, f32[4,1,32,256]{3,2,1,0:T(8,128)S(1)}, u32[]{:S(2)}, u32[]{:S(2)}) collective-permute-start(f32[4,1,32,256]{3,2,1,0:T(8,128)S(1)} %get-tuple-element.18), channel_id=1, source_target_pairs={{8,0},{16,8},{24,16},{9,1},{17,9},{25,17},{10,2},{18,10},{26,18},{... | collective-permute-start | bytes 393224 | tf_op jit(solution)/shard_map/ppermute | solution.py:17
  47.1 11.9 %collective-permute-start.8 = (f32[2,1,32,256]{3,1,2,0:T(1,128)S(1)}, f32[2,1,32,256]{3,1,2,0:T(1,128)S(1)}, u32[]{:S(2)}, u32[]{:S(2)}) collective-permute-start(f32[2,1,32,256]{3,1,2,0:T(1,128)S(1)} %get-tuple-element.68), channel_id=1, source_target_pairs={{8,0},{16,8},{24,16},{9,1},{17,9},{25,17},{10,2},{18,10},{26,18},{... | collective-permute-start | bytes 196616 | tf_op jit(solution)/shard_map/ppermute | solution.py:17
  48.4 10.6 %collective-permute-start.9 = (f32[2,1,32,256]{3,1,2,0:T(1,128)S(1)}, f32[2,1,32,256]{3,1,2,0:T(1,128)S(1)}, u32[]{:S(2)}, u32[]{:S(2)}) collective-permute-start(f32[2,1,32,256]{3,1,2,0:T(1,128)S(1)} %get-tuple-element.67), channel_id=1, source_target_pairs={{0,8},{8,16},{16,24},{1,9},{9,17},{17,25},{2,10},{10,18},{18,26},{... | collective-permute-start | bytes 196616 | tf_op jit(solution)/shard_map/ppermute | solution.py:16
  53.3 12.5 %collective-permute-start.18 = (f32[4,34,1,256]{3,1,2,0:T(8,128)S(1)}, f32[4,34,1,256]{3,1,2,0:T(8,128)S(1)}, u32[]{:S(2)}, u32[]{:S(2)}) collective-permute-start(f32[4,34,1,256]{3,1,2,0:T(8,128)S(1)} %copy.49), channel_id=1, source_target_pairs={{0,1},{1,2},{2,3},{3,4},{4,5},{5,6},{6,7},{8,9},{9,10},{10,11},{11... | collective-permute-start | bytes 417800 | tf_op jit(solution)/shard_map/ppermute | solution.py:16
  57.8 8.2 %collective-permute-start.19 = (f32[4,34,1,256]{3,1,2,0:T(8,128)S(1)}, f32[4,34,1,256]{3,1,2,0:T(8,128)S(1)}, u32[]{:S(2)}, u32[]{:S(2)}) collective-permute-start(f32[4,34,1,256]{3,1,2,0:T(8,128)S(1)} %copy.50), channel_id=1, source_target_pairs={{1,0},{2,1},{3,2},{4,3},{5,4},{6,5},{7,6},{9,8},{10,9},{11,10},{12... | collective-permute-start | bytes 417800 | tf_op jit(solution)/shard_map/ppermute | solution.py:17
  59.1 7.1 %collective-permute-start.10 = (f32[2,34,1,256]{3,1,2,0:T(8,128)S(1)}, f32[2,34,1,256]{3,1,2,0:T(8,128)S(1)}, u32[]{:S(2)}, u32[]{:S(2)}) collective-permute-start(f32[2,34,1,256]{3,1,2,0:T(8,128)S(1)} %get-tuple-element.43), channel_id=1, source_target_pairs={{1,0},{2,1},{3,2},{4,3},{5,4},{6,5},{7,6},{9,8},{10,9},{11,10},{12... | collective-permute-start | bytes 208904 | tf_op jit(solution)/shard_map/ppermute | solution.py:17
  60.4 7.9 %collective-permute-start.11 = (f32[2,34,1,256]{3,1,2,0:T(8,128)S(1)}, f32[2,34,1,256]{3,1,2,0:T(8,128)S(1)}, u32[]{:S(2)}, u32[]{:S(2)}) collective-permute-start(f32[2,34,1,256]{3,1,2,0:T(8,128)S(1)} %get-tuple-element.44), channel_id=1, source_target_pairs={{0,1},{1,2},{2,3},{3,4},{4,5},{5,6},{6,7},{8,9},{9,10},{10,11},{11... | collective-permute-start | bytes 208904 | tf_op jit(solution)/shard_map/ppermute | solution.py:16
  78.7 6.1 %collective-permute-start.14 = (f32[2,34,1,256]{3,1,2,0:T(8,128)S(1)}, f32[2,34,1,256]{3,1,2,0:T(8,128)S(1)}, u32[]{:S(2)}, u32[]{:S(2)}) collective-permute-start(f32[2,34,1,256]{3,1,2,0:T(8,128)S(1)} %get-tuple-element.41), channel_id=1, source_target_pairs={{1,0},{2,1},{3,2},{4,3},{5,4},{6,5},{7,6},{9,8},{10,9},{11,10},{12... | collective-permute-start | bytes 208904 | tf_op jit(solution)/shard_map/ppermute | solution.py:17
  89.6 8.2 %collective-permute-start.20 = (f32[2,1,32,256]{3,1,2,0:T(1,128)S(1)}, f32[2,1,32,256]{3,1,2,0:T(1,128)S(1)}, u32[]{:S(2)}, u32[]{:S(2)}) collective-permute-start(f32[2,1,32,256]{3,1,2,0:T(1,128)S(1)} %get-tuple-element.63), channel_id=1, source_target_pairs={{0,8},{8,16},{16,24},{1,9},{9,17},{17,25},{2,10},{10,18},{18,26},{... | collective-permute-start | bytes 196616 | tf_op jit(solution)/shard_map/ppermute | solution.py:16
  98.3 7.2 %collective-permute-start.22 = (f32[2,34,1,256]{3,1,2,0:T(8,128)S(1)}, f32[2,34,1,256]{3,1,2,0:T(8,128)S(1)}, u32[]{:S(2)}, u32[]{:S(2)}) collective-permute-start(f32[2,34,1,256]{3,1,2,0:T(8,128)S(1)} %get-tuple-element.39), channel_id=1, source_target_pairs={{0,1},{1,2},{2,3},{3,4},{4,5},{5,6},{6,7},{8,9},{9,10},{10,11},{11... | collective-permute-start | bytes 208904 | tf_op jit(solution)/shard_map/ppermute | solution.py:16
  102.6 6.4 %collective-permute-start.23 = (f32[2,34,1,256]{3,1,2,0:T(8,128)S(1)}, f32[2,34,1,256]{3,1,2,0:T(8,128)S(1)}, u32[]{:S(2)}, u32[]{:S(2)}) collective-permute-start(f32[2,34,1,256]{3,1,2,0:T(8,128)S(1)} %get-tuple-element.40), channel_id=1, source_target_pairs={{1,0},{2,1},{3,2},{4,3},{5,4},{6,5},{7,6},{9,8},{10,9},{11,10},{12... | collective-permute-start | bytes 208904 | tf_op jit(solution)/shard_map/ppermute | solution.py:17
  122.1 7.6 %collective-permute-start.26 = (f32[2,34,1,256]{3,1,2,0:T(8,128)S(1)}, f32[2,34,1,256]{3,1,2,0:T(8,128)S(1)}, u32[]{:S(2)}, u32[]{:S(2)}) collective-permute-start(f32[2,34,1,256]{3,1,2,0:T(8,128)S(1)} %get-tuple-element.37), channel_id=1, source_target_pairs={{0,1},{1,2},{2,3},{3,4},{4,5},{5,6},{6,7},{8,9},{9,10},{10,11},{11... | collective-permute-start | bytes 208904 | tf_op jit(solution)/shard_map/ppermute | solution.py:16
  185.8 6.2 %collective-permute-start.39 = (f32[2,34,1,256]{3,1,2,0:T(8,128)S(1)}, f32[2,34,1,256]{3,1,2,0:T(8,128)S(1)}, u32[]{:S(2)}, u32[]{:S(2)}) collective-permute-start(f32[2,34,1,256]{3,1,2,0:T(8,128)S(1)} %get-tuple-element.32), channel_id=1, source_target_pairs={{0,1},{1,2},{2,3},{3,4},{4,5},{5,6},{6,7},{8,9},{9,10},{10,11},{11... | collective-permute-start | bytes 208904 | tf_op jit(solution)/shard_map/ppermute | solution.py:16
  203.5 7.0 %collective-permute-start.43 = (f32[2,34,1,256]{3,1,2,0:T(8,128)S(1)}, f32[2,34,1,256]{3,1,2,0:T(8,128)S(1)}, u32[]{:S(2)}, u32[]{:S(2)}) collective-permute-start(f32[2,34,1,256]{3,1,2,0:T(8,128)S(1)} %get-tuple-element.30), channel_id=1, source_target_pairs={{0,1},{1,2},{2,3},{3,4},{4,5},{5,6},{6,7},{8,9},{9,10},{10,11},{11... | collective-permute-start | bytes 208904 | tf_op jit(solution)/shard_map/ppermute | solution.py:16
  239.1 7.5 %collective-permute-start.50 = (f32[2,34,1,256]{3,1,2,0:T(8,128)S(1)}, f32[2,34,1,256]{3,1,2,0:T(8,128)S(1)}, u32[]{:S(2)}, u32[]{:S(2)}) collective-permute-start(f32[2,34,1,256]{3,1,2,0:T(8,128)S(1)} %get-tuple-element.25), channel_id=1, source_target_pairs={{1,0},{2,1},{3,2},{4,3},{5,4},{6,5},{7,6},{9,8},{10,9},{11,10},{12... | collective-permute-start | bytes 208904 | tf_op jit(solution)/shard_map/ppermute | solution.py:17
  240.4 6.7 %collective-permute-start.51 = (f32[2,34,1,256]{3,1,2,0:T(8,128)S(1)}, f32[2,34,1,256]{3,1,2,0:T(8,128)S(1)}, u32[]{:S(2)}, u32[]{:S(2)}) collective-permute-start(f32[2,34,1,256]{3,1,2,0:T(8,128)S(1)} %get-tuple-element.26), channel_id=1, source_target_pairs={{0,1},{1,2},{2,3},{3,4},{4,5},{5,6},{6,7},{8,9},{9,10},{10,11},{11... | collective-permute-start | bytes 208904 | tf_op jit(solution)/shard_map/ppermute | solution.py:16
  439.6 30.3 %all-to-all-start.1 = ((f32[8,8,32,256]{3,2,1,0:T(8,128)}), f32[8,8,32,256]{3,2,1,0:T(8,128)S(1)}, u32[]{:S(2)}, u32[]{:S(2)}) async-start(f32[8,8,32,256]{3,2,1,0:T(8,128)} %copy.62), calls=%async_computation.1 | async-start | bytes 4194304 | tf_op jit(solution)/shard_map/all_to_all | solution.py:105
  (34 other events, 200.8 us)

commit v2 on v0

v2 whole, which is shorter than its diff:
```python
import functools

import jax
import jax.numpy as jnp
from jax import lax
from jax.experimental import pallas as pl
from jax.experimental.pallas import tpu as pltpu
from jax.sharding import PartitionSpec as P

STEPS = 4
MESH = pl.DeviceIdType.MESH
LANES = 128
C0, PX, MX, PY, MY, PZ, MZ = range(7)


def spread(value, shape):
    return jnp.broadcast_to(value, shape)


def kernel(
    cells,
    probes,
    velocity,
    diffusivity,
    weight,
    basis,
    projected,
    state,
    coef,
    edge_tile,
    edge_row,
    images,
    x_out,
    x_in,
    y_out,
    y_in,
    sums_probe,
    sums_sx,
    sums_sy,
    inverse_ref,
    x_send,
    x_recv,
    y_send,
    y_recv,
    image_send,
    image_recv,
    sum_send,
    sum_recv,
):
    group, nx, ny, nz = probes.shape
    at = {name: lax.axis_index(name) for name in ("probe", "sx", "sy")}
    size = {name: lax.axis_size(name) for name in ("probe", "sx", "sy")}
    me = at["probe"]

    barrier = pltpu.get_barrier_semaphore()
    peers = 0
    for name in ("probe", "sx", "sy"):
        for shift in range(1, size[name]):
            peer = lax.rem(at[name] + shift, size[name])
            pl.semaphore_signal(barrier, inc=1, device_id={name: peer}, device_id_type=MESH)
            peers += 1

    rows = lax.broadcasted_iota(jnp.int32, (ny, nz), 0)
    cols = lax.broadcasted_iota(jnp.int32, (ny, nz), 1)
    tile_rows = lax.broadcasted_iota(jnp.int32, (8, nz), 0)
    zero = jnp.zeros((ny, nz), jnp.float32)

    def prepare(x, carry):
        k = diffusivity[x]
        hx, hy, hz = (0.5 * velocity[d, x] for d in range(3))
        coef[C0, x + 1] = 1.0 - 6.0 * k
        coef[PX, x + 1] = k - hx
        coef[MX, x + 1] = k + hx
        plus, minus = k - hy, k + hy
        coef[PY, x + 1] = jnp.where(rows == ny - 1, 0.0, plus)
        coef[MY, x + 1] = jnp.where(rows == 0, 0.0, minus)
        edge_tile[0, x] = jnp.where(tile_rows == 0, minus[0:8], 0.0)
        edge_tile[1, x] = jnp.where(tile_rows == 7, plus[ny - 8 : ny], 0.0)
        edge_row[0, x] = minus[0:1]
        edge_row[1, x] = plus[ny - 1 : ny]
        coef[PZ, x + 1] = jnp.where(cols == nz - 1, 0.0, k - hz)
        coef[MZ, x + 1] = jnp.where(cols == 0, 0.0, k + hz)
        for p in range(group):
            state[0, p, x + 1] = probes[p, x]
        return carry

    lax.fori_loop(0, nx, prepare, 0)
    for x in (0, nx + 1):
        coef[PX, x] = zero
        coef[MX, x] = zero
        for slot in range(2):
            for p in range(group):
                state[slot, p, x] = zero

    pl.semaphore_wait(barrier, peers)

    has = {}
    for name in ("sx", "sy"):
        has[name] = (at[name] > 0, at[name] < size[name] - 1)

    def face(name, side, slot):
        out, into = (x_out, x_in) if name == "sx" else (y_out, y_in)
        send, recv = (x_send, x_recv) if name == "sx" else (y_send, y_recv)
        step = 1 if side else -1
        return pltpu.make_async_remote_copy(
            src_ref=out.at[side],
            dst_ref=into.at[slot, 1 - side],
            send_sem=send.at[side],
            recv_sem=recv.at[slot, 1 - side],
            device_id={name: at[name] + step},
            device_id_type=MESH,
        )

    def arriving(name, side, slot):
        into = x_in if name == "sx" else y_in
        out = x_out if name == "sx" else y_out
        send, recv = (x_send, x_recv) if name == "sx" else (y_send, y_recv)
        step = 1 if side else -1
        return pltpu.make_async_remote_copy(
            src_ref=out.at[side],
            dst_ref=into.at[slot, side],
            send_sem=send.at[side],
            recv_sem=recv.at[slot, side],
            device_id={name: at[name] + step},
            device_id_type=MESH,
        )

    def fill(now, adjoint):
        def one(x, carry):
            for p in range(group):
                low = state[now, p, x + 1, 0:1, :]
                high = state[now, p, x + 1, ny - 1 : ny, :]
                if adjoint:
                    low = low * edge_row[0, x]
                    high = high * edge_row[1, x]
                y_out[0, p, x] = low
                y_out[1, p, x] = high
            return carry

        lax.fori_loop(0, nx, one, 0)
        for p in range(group):
            low, high = state[now, p, 1], state[now, p, nx]
            if adjoint:
                low, high = low * coef[MX, 1], high * coef[PX, nx]
            x_out[0, p] = low
            x_out[1, p] = high

    def local(now, later, adjoint):
        def plane(x, carry):
            for p in range(group):
                u = state[now, p, x]
                before, after = state[now, p, x - 1], state[now, p, x + 1]
                if adjoint:
                    r = coef[C0, x] * u
                    r = r + coef[PX, x - 1] * before + coef[MX, x + 1] * after
                    r = r + pltpu.roll(coef[PY, x] * u, 1, 0)
                    r = r + pltpu.roll(coef[MY, x] * u, ny - 1, 0)
                    r = r + pltpu.roll(coef[PZ, x] * u, 1, 1)
                    r = r + pltpu.roll(coef[MZ, x] * u, nz - 1, 1)
                else:
                    r = coef[C0, x] * u
                    r = r + coef[PX, x] * after + coef[MX, x] * before
                    r = r + coef[PY, x] * pltpu.roll(u, ny - 1, 0)
                    r = r + coef[MY, x] * pltpu.roll(u, 1, 0)
                    r = r + coef[PZ, x] * pltpu.roll(u, nz - 1, 1)
                    r = r + coef[MZ, x] * pltpu.roll(u, 1, 1)
                state[later, p, x] = r
            return carry

        lax.fori_loop(1, nx + 1, plane, 0)

    def fix_x(later, slot, side, adjoint):
        x = nx if side else 1
        for p in range(group):
            got = x_in[slot, side, p]
            if not adjoint:
                got = got * coef[PX if side else MX, x]
            state[later, p, x] = state[later, p, x] + got

    def fix_y(later, slot, side, adjoint):
        first = ny - 8 if side else 0

        def one(x, carry):
            for p in range(group):
                got = spread(y_in[slot, side, p, x], (8, nz))
                if adjoint:
                    got = jnp.where(tile_rows == (7 if side else 0), got, 0.0)
                else:
                    got = got * edge_tile[side, x]
                tile = state[later, p, x + 1, first : first + 8, :]
                state[later, p, x + 1, first : first + 8, :] = tile + got
            return carry

        lax.fori_loop(0, nx, one, 0)

    def steps(adjoint):
        def step(i, carry):
            now = lax.rem(i, 2)
            later = 1 - now
            fill(now, adjoint)
            for name in ("sy", "sx"):
                for side in range(2):

                    @pl.when(has[name][side])
                    def _():
                        face(name, side, now).start()

            local(now, later, adjoint)
            for name in ("sx", "sy"):
                for side in range(2):

                    @pl.when(has[name][side])
                    def _():
                        face(name, side, now).wait_send()
                        arriving(name, side, now).wait_recv()
                        if name == "sx":
                            fix_x(later, now, side, adjoint)
                        else:
                            fix_y(later, now, side, adjoint)

            return carry

        lax.fori_loop(0, STEPS, step, 0)

    def apply():
        steps(False)

        def scale(x, carry):
            for p in range(group):
                state[0, p, x + 1] = state[0, p, x + 1] * weight[x]
            return carry

        lax.fori_loop(0, nx, scale, 0)
        steps(True)

    def image_copy(pair, target, sem):
        return pltpu.make_async_remote_copy(
            src_ref=images.at[pl.ds(group * pair, group)],
            dst_ref=images.at[pl.ds(group * pair, group)],
            send_sem=image_send.at[sem],
            recv_sem=image_recv.at[pair],
            device_id={"probe": target},
            device_id_type=MESH,
        )

    apply()

    def keep(x, carry):
        for p in range(group):
            images[group * me + p, x] = state[0, p, x + 1]
        return carry

    lax.fori_loop(0, nx, keep, 0)

    @pl.when(me == 0)
    def _():
        image_copy(0, 2, 1).start()
        image_copy(0, 1, 0).start()

    @pl.when(me == 1)
    def _():
        image_copy(1, 3, 0).start()

    @pl.when(me == 2)
    def _():
        image_copy(2, 3, 0).start()

    apply()

    @pl.when(me == 0)
    def _():
        image_copy(0, 2, 1).wait_send()
        image_copy(0, 1, 0).wait_send()

    @pl.when(me == 1)
    def _():
        image_copy(1, 3, 0).wait_send()
        image_copy(0, 2, 1).wait_recv()

    @pl.when(me == 2)
    def _():
        image_copy(0, 3, 1).wait_recv()
        image_copy(0, 3, 1).start()
        image_copy(1, 3, 1).wait_recv()
        image_copy(2, 3, 0).wait_send()
        image_copy(0, 3, 1).wait_send()

    @pl.when(me == 3)
    def _():
        image_copy(1, 2, 0).wait_recv()
        image_copy(1, 2, 0).start()
        image_copy(2, 2, 0).wait_recv()
        image_copy(0, 2, 0).wait_recv()
        image_copy(1, 2, 0).wait_send()

    trow = lax.broadcasted_iota(jnp.int32, (8, LANES), 0)
    tcol = lax.broadcasted_iota(jnp.int32, (8, LANES), 1)
    count = size["probe"] * group

    def inner(k, total):
        def plane(x, acc):
            own = [images[group * me + j, x] for j in range(group)]
            second = [state[0, j, x + 1] for j in range(group)]
            acc = list(acc)
            for i in range(group):
                other = images[group * k + i, x]
                for j in range(group):
                    for m, right in enumerate((own[j], second[j])):
                        n = (i * group + j) * 2 + m
                        prod = other * right
                        for y in range(0, ny, 8):
                            acc[n] = acc[n] + prod[y : y + 8]
            return tuple(acc)

        start = tuple(jnp.zeros((8, nz), jnp.float32) for _ in range(group * group * 2))
        acc = lax.fori_loop(0, nx, plane, start)
        for i in range(group):
            for j in range(group):
                for m in range(2):
                    value = jnp.sum(acc[(i * group + j) * 2 + m])
                    low, high = group * k + i, group * me + j
                    here = jnp.logical_and(trow == low, tcol == high + count * m)
                    there = jnp.logical_and(trow == high, tcol == low + count * m)
                    there = jnp.logical_and(there, k < me)
                    total = jnp.where(jnp.logical_or(here, there), value, total)
        return total

    total = lax.fori_loop(0, me + 1, inner, jnp.zeros((8, LANES), jnp.float32))

    sem = 0
    for name, sums in (("probe", sums_probe), ("sx", sums_sx), ("sy", sums_sy)):
        mine = at[name]
        sums[mine] = total

        def part(shift, sem):
            return pltpu.make_async_remote_copy(
                src_ref=sums.at[mine],
                dst_ref=sums.at[mine],
                send_sem=sum_send.at[sem],
                recv_sem=sum_recv.at[sem],
                device_id={name: lax.rem(mine + shift, size[name])},
                device_id_type=MESH,
            )

        for shift in range(1, size[name]):
            part(shift, sem + shift - 1).start()
        for shift in range(1, size[name]):
            part(shift, sem + shift - 1).wait()
        sem += size[name] - 1
        total = sums[0]
        for other in range(1, size[name]):
            total = total + sums[other]

    full = (8, LANES)
    work = total / cells
    work = jnp.where(tcol == trow + 2 * count, 1.0, work)
    for j in range(count):
        pivot_row = spread(work[j : j + 1, :], full)
        column = spread(work[:, j : j + 1], full)
        pivot = spread(work[j : j + 1, j : j + 1], full)
        work = work - jnp.where(trow > j, column / pivot, 0.0) * pivot_row
    diagonal = jnp.sum(jnp.where(trow == tcol, work, 0.0), axis=1, keepdims=True)
    work = work / spread(jnp.sqrt(diagonal), full)
    inverse = jnp.where(tcol < count, pltpu.roll(work, LANES - 2 * count, 1), 0.0)
    half = jnp.where(tcol < count, pltpu.roll(work, LANES - count, 1), 0.0)
    product = lax.dot_general(
        half,
        inverse,
        (((1,), (1,)), ((), ())),
        precision=lax.Precision.HIGHEST,
        preferred_element_type=jnp.float32,
    )
    projected[...] = product
    inverse_ref[...] = inverse

    for g in range(size["probe"]):

        @pl.when(me == g)
        def _():
            inv = inverse_ref[...]
            factor = [
                [
                    jnp.sum(jnp.where((trow == group * g + r) & (tcol == i), inv, 0.0))
                    for i in range(group * g + r + 1)
                ]
                for r in range(group)
            ]

            def plane(x, carry):
                field = [images[i, x] for i in range(group * (g + 1))]
                for r in range(group):
                    out = factor[r][0] * field[0]
                    for i in range(1, group * g + r + 1):
                        out = out + factor[r][i] * field[i]
                    basis[r, x] = out
                return carry

            lax.fori_loop(0, nx, plane, 0)


def shards(probes, velocity, diffusivity, obs_weight):
    group, nx, ny, nz = probes.shape
    nprobe, nsx, nsy = (lax.axis_size(name) for name in ("probe", "sx", "sy"))
    count = group * nprobe
    cells = float(nx * nsx * ny * nsy * nz)
    vmem = pl.BlockSpec(memory_space=pltpu.VMEM)
    f32 = jnp.float32
    total = nprobe + nsx + nsy - 3
    return pl.pallas_call(
        functools.partial(kernel, cells),
        out_shape=(
            jax.ShapeDtypeStruct(probes.shape, f32),
            jax.ShapeDtypeStruct((count, count), f32),
        ),
        in_specs=[vmem] * 4,
        out_specs=(vmem, vmem),
        scratch_shapes=[
            pltpu.VMEM((2, group, nx + 2, ny, nz), f32),
            pltpu.VMEM((7, nx + 2, ny, nz), f32),
            pltpu.VMEM((2, nx, 8, nz), f32),
            pltpu.VMEM((2, nx, 1, nz), f32),
            pltpu.VMEM((count, nx, ny, nz), f32),
            pltpu.VMEM((2, group, ny, nz), f32),
            pltpu.VMEM((2, 2, group, ny, nz), f32),
            pltpu.VMEM((2, group, nx, 1, nz), f32),
            pltpu.VMEM((2, 2, group, nx, 1, nz), f32),
            pltpu.VMEM((nprobe, 8, LANES), f32),
            pltpu.VMEM((nsx, 8, LANES), f32),
            pltpu.VMEM((nsy, 8, LANES), f32),
            pltpu.VMEM((8, LANES), f32),
            pltpu.SemaphoreType.DMA((2,)),
            pltpu.SemaphoreType.DMA((2, 2)),
            pltpu.SemaphoreType.DMA((2,)),
            pltpu.SemaphoreType.DMA((2, 2)),
            pltpu.SemaphoreType.DMA((2,)),
            pltpu.SemaphoreType.DMA((nprobe,)),
            pltpu.SemaphoreType.DMA((total,)),
            pltpu.SemaphoreType.DMA((total,)),
        ],
        compiler_params=pltpu.CompilerParams(
            collective_id=0, has_side_effects=True, vmem_limit_bytes=60 * 1024 * 1024
        ),
    )(probes, velocity, diffusivity, obs_weight)


def solution(mesh):
    return jax.shard_map(
        shards,
        mesh=mesh,
        in_specs=(
            P("probe", "sx", "sy", None),
            P(None, "sx", "sy", None),
            P("sx", "sy", None),
            P("sx", "sy", None),
        ),
        out_specs=(P("probe", "sx", "sy", None), P()),
        check_vma=False,
    )
```

time: 634 us -> 174 us (0.27); the launches traced: 624 us -> 173 us
  blocking collectives: 204 us -> 0 us
  starting transfers between devices: 193 us -> 0 us
  Pallas kernels: 0 us -> 168 us
  waiting for transfers between devices: 111 us -> 0 us
  other arithmetic: 60.5 us -> 0 us
  local copies, waits for them, and re-layouts: 35.1 us -> 3.76 us
  matrix products: 16.6 us -> 0 us
    pallas_call x0 -> x1, Pallas kernels: none -> 168 us  [shards(): pl.pallas_call(functools.partial(kernel, cells), out_shape=(jax.ShapeDtyp...]
    ppermute x68 -> x0, starting transfers between devices: 166 us -> none  [the longest x34 122 us: extended(): before = lax.ppermute(last, axis, up)]
    psum x2 -> x0, blocking collectives: 126 us -> none  [the longest x1 62.9 us: shards(): gram = lax.psum(partial_gram, ('probe', 'sx', 'sy')) / ncells]
    ppermute x68 -> x0, waiting for transfers between devices: 87.8 us -> none  [the longest x34 78.5 us: extended(): after = lax.ppermute(leading, axis, down)]
    all_to_all x2 -> x0, blocking collectives: 78.8 us -> none  [the longest x1 49 us: shards(): lax.all_to_all(images, 'probe', split_axis=1, concat_axis=0, tiled=True)]
    mul x19 -> x0, other arithmetic: 27.2 us -> none  [the longest x8 22.5 us: adjoint_step(): (cc[0] + 0.5 * cc[3]) * inner]
    all_to_all x1 -> x0, starting transfers between devices: 27 us -> none  [shards(): lax.all_to_all(second, 'probe', split_axis=1, concat_axis=0, tiled=True)]
    add x8 -> x0, other arithmetic: 25.5 us -> none  [the longest x6 20.2 us: forward_step(): result + (spread - 0.5 * cc[3]) * padded[..., 2:]]
  transfers between devices with their start and end apart: 69 -> 0, of which waited for: 30 -> 0; matrix products, arithmetic and copies ran while one was open for 4% -> 0% of each run, Pallas kernels for 0% -> 0%
where the time goes in v2:
time: 174 us; the launch traced here: 173 us
  Pallas kernels  168 us (97%)
  local copies, waits for them, and re-layouts  3.76 us (2%)
    pallas_call x1, Pallas kernels, shards(): pl.pallas_call(functools.partial(kernel, cells), out_shape=(jax.ShapeDtyp...  168 us
    unnamed x4, local copies, waits for them, and re-layouts  3.76 us

profile of v2, /device:TPU:1, one launch (start us, length us, event | category | flops | bytes accessed | tf_op | source)
XLA Modules:
  0.0 172.6 jit_solution(10271245646590387738)
XLA Ops:
  0.6 168.2 %shard_map.59 = (f32[2,32,32,256]{3,2,1,0:T(8,128)}, f32[8,8]{1,0:T(8,128)}) custom-call(f32[2,32,32,256]{3,2,1,0:T(8,128)} %probes.1, f32[3,32,32,256]{3,2,1,0:T(8,128)} %velocity.1, f32[32,32,256]{2,1,0:T(8,128)} %diffusivity.1, f32[32,32,256]{2,1,0:T(8,128)} %weight.1), custom_call_target="tpu_custom_call" | custom-call | tf_op jit(solution)/shard_map/pallas_call | solution.py:409
  168.8 0.0 copy-start
  168.8 3.2 %copy.8 = f32[2,32,32,256]{3,2,1,0:T(8,128)} copy(f32[2,32,32,256]{3,2,1,0:T(8,128)} %get-tuple-element.4) | data formatting | bytes 4194304
  172.0 0.0 copy-done
  172.0 0.6 copy.9
Async XLA Ops:
  168.8 3.2 %copy-start = (f32[8,8]{1,0:T(8,128)S(1)}, f32[8,8]{1,0:T(8,128)}, u32[]{:S(2)}) copy-start(f32[8,8]{1,0:T(8,128)} %get-tuple-element.5) | copy-start | bytes 772

commit v3 on v2

v3 whole, which is shorter than its diff:
```python
import functools

import jax
import jax.numpy as jnp
from jax import lax
from jax.experimental import pallas as pl
from jax.experimental.pallas import tpu as pltpu
from jax.sharding import PartitionSpec as P

STEPS = 4
UNROLL = 1
MESH = pl.DeviceIdType.MESH
LANES = 128
C0, PX, MX, PY, MY, PZ, MZ = range(7)


def spread(value, shape):
    return jnp.broadcast_to(value, shape)


def kernel(
    cells,
    probes,
    velocity,
    diffusivity,
    weight,
    basis,
    projected,
    field,
    other_field,
    center,
    coef,
    edge,
    got_probes,
    got_velocity,
    got_diffusivity,
    got_weight,
    images,
    x_in,
    y_out,
    y_in,
    sums_probe,
    sums_sx,
    sums_sy,
    inverse_ref,
    x_send,
    x_recv,
    y_send,
    y_recv,
    edge_send,
    edge_recv,
    image_send,
    image_recv,
    sum_send,
    sum_recv,
    in_sem,
    out_sem,
):
    group, nx, ny, nz = probes.shape
    deep, wide = ny // 8, nz // LANES
    at = {name: lax.axis_index(name) for name in ("probe", "sx", "sy")}
    size = {name: lax.axis_size(name) for name in ("probe", "sx", "sy")}
    me = at["probe"]
    has = {name: (at[name] > 0, at[name] < size[name] - 1) for name in ("sx", "sy")}

    def tile(t):
        return slice(t * LANES, (t + 1) * LANES)

    parts = 4 if nx % 4 == 0 else 1
    per = nx // parts

    def moved(ref, lead, part, t):
        return ref.at[lead + (pl.ds(part * per, per), slice(None), pl.ds(t * LANES, LANES))]

    def held(ref, lead, part, t):
        return ref.at[lead + (pl.ds(part * per, per), t)]

    arriving = {}
    for part in range(parts):
        for n, (src, dst, lead) in enumerate(
            (
                (diffusivity, got_diffusivity, ()),
                (velocity, got_velocity, (slice(None),)),
                (probes, got_probes, (slice(None),)),
                (weight, got_weight, ()),
            )
        ):
            for t in range(wide):
                copy = pltpu.make_async_copy(
                    moved(src, lead, part, t), held(dst, lead, part, t), in_sem.at[part, n, t]
                )
                arriving[part, n, t] = copy
                copy.start()

    def rows_of(ref, index, l, t):
        return ref[index + (t, pl.ds(l, 8, stride=deep), slice(None))]

    srow = lax.broadcasted_iota(jnp.int32, (8, LANES), 0)
    lane = lax.broadcasted_iota(jnp.int32, (8, LANES), 1)
    zero = jnp.zeros((8, LANES), jnp.float32)

    def shift_z(tiles, up):
        rolled = [pltpu.roll(v, LANES - 1 if up else 1, 1) for v in tiles]
        out = []
        for t in range(wide):
            other = t + 1 if up else t - 1
            if 0 <= other < wide:
                out.append(jnp.where(lane == (LANES - 1 if up else 0), rolled[other], rolled[t]))
            else:
                out.append(rolled[t])
        return out

    def shift_y(tiles, l, up):
        if up:
            return tiles[l + 1] if l + 1 < deep else pltpu.roll(tiles[0], 7, 0)
        return tiles[l - 1] if l > 0 else pltpu.roll(tiles[deep - 1], 1, 0)

    for x in (0, nx + 1):
        for l in range(deep):
            for t in range(wide):
                for ref in (field, other_field):
                    for p in range(group):
                        ref[p, x, l, :, tile(t)] = zero
    for l in range(deep):
        for t in range(wide):
            coef[1, MX, 1, l, :, tile(t)] = zero
            coef[1, PX, nx, l, :, tile(t)] = zero

    barrier = pltpu.get_barrier_semaphore()
    peers = 0
    for name in ("probe", "sx", "sy"):
        for shift in range(1, size[name]):
            peer = lax.rem(at[name] + shift, size[name])
            pl.semaphore_signal(barrier, inc=1, device_id={name: peer}, device_id_type=MESH)
            peers += 1

    def prepare(x, carry):
        last, first = nz - LANES, 0
        plus_y, minus_y = [], []
        for t in range(wide):
            plus_y.append([])
            minus_y.append([])
            for l in range(deep):
                k = rows_of(got_diffusivity, (x,), l, t)
                hx, hy = (0.5 * rows_of(got_velocity, (d, x), l, t) for d in range(2))
                center[x + 1, l, :, tile(t)] = 1.0 - 6.0 * k
                coef[0, PX, x + 1, l, :, tile(t)] = k - hx
                coef[0, MX, x + 1, l, :, tile(t)] = k + hx
                coef[1, MX, x + 2, l, :, tile(t)] = k - hx
                coef[1, PX, x, l, :, tile(t)] = k + hx
                plus_y[t].append(k - hy)
                minus_y[t].append(k + hy)
                for p in range(group):
                    field[p, x + 1, l, :, tile(t)] = rows_of(got_probes, (p, x), l, t)
            edge[0, 0, x, :, tile(t)] = minus_y[t][0][0:1]
            edge[0, 1, x, :, tile(t)] = plus_y[t][deep - 1][7:8]
            for l in range(deep):
                up, down = shift_y(minus_y[t], l, True), shift_y(plus_y[t], l, False)
                plus, minus = plus_y[t][l], minus_y[t][l]
                if l == deep - 1:
                    up, plus = (jnp.where(srow == 7, 0.0, v) for v in (up, plus))
                if l == 0:
                    down, minus = (jnp.where(srow == 0, 0.0, v) for v in (down, minus))
                coef[0, PY, x + 1, l, :, tile(t)] = plus
                coef[0, MY, x + 1, l, :, tile(t)] = minus
                coef[1, PY, x + 1, l, :, tile(t)] = up
                coef[1, MY, x + 1, l, :, tile(t)] = down
        for l in range(deep):
            ks = [rows_of(got_diffusivity, (x,), l, t) for t in range(wide)]
            hs = [0.5 * rows_of(got_velocity, (2, x), l, t) for t in range(wide)]
            plus = [k - h for k, h in zip(ks, hs)]
            minus = [k + h for k, h in zip(ks, hs)]
            up, down = shift_z(minus, True), shift_z(plus, False)
            for v in (plus, up):
                v[wide - 1] = jnp.where(lane == LANES - 1, 0.0, v[wide - 1])
            for v in (minus, down):
                v[0] = jnp.where(lane == 0, 0.0, v[0])
            for t in range(wide):
                coef[0, PZ, x + 1, l, :, tile(t)] = plus[t]
                coef[0, MZ, x + 1, l, :, tile(t)] = minus[t]
                coef[1, PZ, x + 1, l, :, tile(t)] = up[t]
                coef[1, MZ, x + 1, l, :, tile(t)] = down[t]
        return carry

    for part in range(parts):
        for n in range(3):
            for t in range(wide):
                arriving[part, n, t].wait()
        lax.fori_loop(part * per, (part + 1) * per, prepare, 0)

    def fill():
        def one(x, carry):
            for p in range(group):
                for t in range(wide):
                    y_out[0, p, x, :, tile(t)] = field[p, x + 1, 0, 0:1, tile(t)]
                    y_out[1, p, x, :, tile(t)] = field[p, x + 1, deep - 1, 7:8, tile(t)]
            return carry

        lax.fori_loop(0, nx, one, 0)

    fill()
    pl.semaphore_wait(barrier, peers)

    def remote(src, dst, send, recv, name, target):
        return pltpu.make_async_remote_copy(
            src_ref=src,
            dst_ref=dst,
            send_sem=send,
            recv_sem=recv,
            device_id={name: target},
            device_id_type=MESH,
        )

    def edges(name, side, came):
        n = 0 if name == "sx" else 1
        into = side if came else 1 - side
        if name == "sx":
            src = coef.at[0, PX, nx] if side else coef.at[0, MX, 1]
            dst = coef.at[1, PX, nx] if into else coef.at[1, MX, 1]
        else:
            src, dst = edge.at[0, side], edge.at[1, into]
        target = at[name] + (1 if side else -1)
        return remote(src, dst, edge_send.at[n, side], edge_recv.at[n, into], name, target)

    def face(name, side, now, came=False):
        into = side if came else 1 - side
        target = at[name] + (1 if side else -1)
        if name == "sx":
            ref = other_field if now else field
            src, dst = ref.at[:, nx if side else 1], x_in.at[now, into]
            return remote(src, dst, x_send.at[side], x_recv.at[now, into], name, target)
        src, dst = y_out.at[side], y_in.at[now, into]
        return remote(src, dst, y_send.at[side], y_recv.at[now, into], name, target)

    def local(old, new, mode):
        def plane(x, carry):
            for p in range(group):
                u = [[old[p, x, l, :, tile(t)] for t in range(wide)] for l in range(deep)]
                by_tile = [[u[l][t] for l in range(deep)] for t in range(wide)]
                for l in range(deep):
                    up_z, down_z = shift_z(u[l], True), shift_z(u[l], False)
                    for t in range(wide):
                        w = tile(t)
                        r = center[x, l, :, w] * u[l][t]
                        r = r + (
                            coef[mode, PX, x, l, :, w] * old[p, x + 1, l, :, w]
                            + coef[mode, MX, x, l, :, w] * old[p, x - 1, l, :, w]
                        )
                        r = r + (
                            coef[mode, PY, x, l, :, w] * shift_y(by_tile[t], l, True)
                            + coef[mode, MY, x, l, :, w] * shift_y(by_tile[t], l, False)
                        )
                        r = r + (
                            coef[mode, PZ, x, l, :, w] * up_z[t]
                            + coef[mode, MZ, x, l, :, w] * down_z[t]
                        )
                        new[p, x, l, :, w] = r
            return carry

        lax.fori_loop(1, nx + 1, plane, 0, unroll=UNROLL)

    def fix_x(slot, new, side, mode):
        x = nx if side else 1
        for l in range(deep):
            for t in range(wide):
                w = tile(t)
                c = coef[mode, PX if side else MX, x, l, :, w]
                for p in range(group):
                    add = c * x_in[slot, side, p, l, :, w]
                    new[p, x, l, :, w] = new[p, x, l, :, w] + add

    def fix_y(slot, new, side, mode):
        l, row = (deep - 1, 7) if side else (0, 0)

        def one(x, carry):
            for t in range(wide):
                w = tile(t)
                c = spread(edge[mode, side, x, :, w], (8, LANES))
                for p in range(group):
                    add = c * spread(y_in[slot, side, p, x, :, w], (8, LANES))
                    v = new[p, x + 1, l, :, w] + jnp.where(srow == row, add, 0.0)
                    new[p, x + 1, l, :, w] = v
                    y_out[side, p, x, :, w] = v[row : row + 1]
            return carry

        lax.fori_loop(0, nx, one, 0, unroll=4)

    chunks = 2 * STEPS
    thick = nx // chunks if nx >= chunks else nx

    def image_copy(pair, target, sem, chunk=None):
        lead = pl.ds(group * pair, group)
        if chunk is None:
            ref, recv, send = images.at[lead], image_recv.at[pair, 0], image_send.at[sem, 0]
        else:
            ref = images.at[lead, pl.ds(chunk * thick, thick)]
            recv, send = image_recv.at[pair, chunk], image_send.at[sem, chunk]
        return remote(ref, ref, send, recv, "probe", target)

    def relay(chunk):
        @pl.when(me == 2)
        def _():
            image_copy(0, 3, 1, chunk).wait_recv()
            image_copy(0, 3, 1, chunk).start()

        @pl.when(me == 3)
        def _():
            image_copy(1, 2, 1, chunk).wait_recv()
            image_copy(1, 2, 1, chunk).start()

    def run(second):
        def step(i, now, mode):
            old, new = (other_field, field) if now else (field, other_field)
            for name in ("sy", "sx"):
                for side in range(2):

                    @pl.when(has[name][side])
                    def _():
                        face(name, side, now).start()

            if second:

                @pl.when(me < 2)
                def _():
                    image_copy(me, me + 2, 1, i).start()

            local(old, new, mode)
            if second:

                @pl.when(i >= 2)
                def _():
                    relay(i - 2)

            for name in ("sx", "sy"):
                for side in range(2):

                    @pl.when(has[name][side])
                    def _():
                        face(name, side, now).wait_send()
                        face(name, side, now, True).wait_recv()
                        (fix_x if name == "sx" else fix_y)(now, new, side, mode)

        def both(i, carry):
            mode = 2 * i // STEPS
            step(2 * i, 0, mode)
            step(2 * i + 1, 1, mode)

            @pl.when(2 * i == STEPS - 2)
            def _():
                def weigh(x, carry):
                    for l in range(deep):
                        for t in range(wide):
                            w = tile(t)
                            c = rows_of(got_weight, (x,), l, t)
                            for p in range(group):
                                v = c * field[p, x + 1, l, :, w]
                                field[p, x + 1, l, :, w] = v
                                if l == 0:
                                    y_out[0, p, x, :, w] = v[0:1]
                                if l == deep - 1:
                                    y_out[1, p, x, :, w] = v[7:8]
                    return carry

                lax.fori_loop(0, nx, weigh, 0)
                if not second:
                    for name in ("sx", "sy"):
                        for side in range(2):

                            @pl.when(has[name][side])
                            def _():
                                edges(name, side, False).wait_send()
                                edges(name, side, True).wait_recv()

            return carry

        lax.fori_loop(0, STEPS, both, 0)

    for name in ("sx", "sy"):
        for side in range(2):

            @pl.when(has[name][side])
            def _():
                edges(name, side, False).start()

    for part in range(parts):
        for t in range(wide):
            arriving[part, 3, t].wait()

    run(False)

    def keep(x, carry):
        for p in range(group):
            images[group * me + p, x] = field[p, x + 1]
        return carry

    lax.fori_loop(0, nx, keep, 0)


    @pl.when(me == 0)
    def _():
        image_copy(0, 1, 0).start()

    @pl.when(me == 2)
    def _():
        image_copy(2, 3, 0).start()

    run(True)

    for chunk in range(chunks - 2, chunks):
        relay(chunk)

    @pl.when(me == 0)
    def _():
        image_copy(0, 1, 0).wait_send()
        for chunk in range(chunks):
            image_copy(0, 2, 1, chunk).wait_send()

    @pl.when(me == 1)
    def _():
        image_copy(0, 2, 1).wait_recv()
        for chunk in range(chunks):
            image_copy(1, 3, 1, chunk).wait_send()

    @pl.when(me == 2)
    def _():
        image_copy(2, 3, 0).wait_send()
        for chunk in range(chunks):
            image_copy(0, 3, 1, chunk).wait_send()
            image_copy(1, 3, 1, chunk).wait_recv()

    @pl.when(me == 3)
    def _():
        image_copy(2, 2, 0).wait_recv()
        for chunk in range(chunks):
            image_copy(1, 2, 1, chunk).wait_send()
            image_copy(0, 2, 1, chunk).wait_recv()

    trow, tcol = srow, lane
    count = size["probe"] * group

    def inner(k, total):
        def plane(x, acc):
            acc = list(acc)
            for l in range(deep):
                own = [images[group * me + j, x, l] for j in range(group)]
                second = [field[j, x + 1, l] for j in range(group)]
                for i in range(group):
                    other = images[group * k + i, x, l]
                    for j in range(group):
                        for m, right in enumerate((own[j], second[j])):
                            n = (i * group + j) * 2 + m
                            acc[n] = acc[n] + other * right
            return tuple(acc)

        start = tuple(jnp.zeros((8, nz), jnp.float32) for _ in range(group * group * 2))
        acc = lax.fori_loop(0, nx, plane, start)
        for i in range(group):
            for j in range(group):
                for m in range(2):
                    value = jnp.sum(acc[(i * group + j) * 2 + m])
                    low, high = group * k + i, group * me + j
                    here = jnp.logical_and(trow == low, tcol == high + count * m)
                    there = jnp.logical_and(trow == high, tcol == low + count * m)
                    there = jnp.logical_and(there, k < me)
                    total = jnp.where(jnp.logical_or(here, there), value, total)
        return total

    total = lax.fori_loop(0, me + 1, inner, zero)

    sem = 0
    for name, sums in (("probe", sums_probe), ("sx", sums_sx), ("sy", sums_sy)):
        mine = at[name]
        sums[mine] = total

        def part(shift, sem):
            return pltpu.make_async_remote_copy(
                src_ref=sums.at[mine],
                dst_ref=sums.at[mine],
                send_sem=sum_send.at[sem],
                recv_sem=sum_recv.at[sem],
                device_id={name: lax.rem(mine + shift, size[name])},
                device_id_type=MESH,
            )

        for shift in range(1, size[name]):
            part(shift, sem + shift - 1).start()
        for shift in range(1, size[name]):
            part(shift, sem + shift - 1).wait()
        sem += size[name] - 1
        total = sums[0]
        for other in range(1, size[name]):
            total = total + sums[other]

    full = (8, LANES)
    work = total / cells
    work = jnp.where(tcol == trow + 2 * count, 1.0, work)
    for j in range(count):
        pivot_row = spread(work[j : j + 1, :], full)
        column = spread(work[:, j : j + 1], full)
        pivot = spread(work[j : j + 1, j : j + 1], full)
        work = work - jnp.where(trow > j, column / pivot, 0.0) * pivot_row
    diagonal = jnp.sum(jnp.where(trow == tcol, work, 0.0), axis=1, keepdims=True)
    work = work / spread(jnp.sqrt(diagonal), full)
    inverse = jnp.where(tcol < count, pltpu.roll(work, LANES - 2 * count, 1), 0.0)
    half = jnp.where(tcol < count, pltpu.roll(work, LANES - count, 1), 0.0)
    product = lax.dot_general(
        half,
        inverse,
        (((1,), (1,)), ((), ())),
        precision=lax.Precision.HIGHEST,
        preferred_element_type=jnp.float32,
    )
    projected[...] = product
    inverse_ref[...] = inverse

    def leaving(part, t):
        whole = (slice(None),)
        return pltpu.make_async_copy(
            held(got_probes, whole, part, t), moved(basis, whole, part, t), out_sem.at[part, t]
        )

    for g in range(size["probe"]):

        @pl.when(me == g)
        def _():
            inv = inverse_ref[...]
            factor = [
                [
                    jnp.sum(jnp.where((trow == group * g + r) & (tcol == i), inv, 0.0))
                    for i in range(group * g + r + 1)
                ]
                for r in range(group)
            ]

            def plane(x, carry):
                for l in range(deep):
                    for t in range(wide):
                        part_of = [images[i, x, l, :, tile(t)] for i in range(group * (g + 1))]
                        for r in range(group):
                            out = factor[r][0] * part_of[0]
                            for i in range(1, group * g + r + 1):
                                out = out + factor[r][i] * part_of[i]
                            got_probes[r, x, t, pl.ds(l, 8, stride=deep), :] = out
                return carry

            for part in range(parts):
                lax.fori_loop(part * per, (part + 1) * per, plane, 0)
                for t in range(wide):
                    leaving(part, t).start()

    for part in range(parts):
        for t in range(wide):
            leaving(part, t).wait()


def shards(probes, velocity, diffusivity, obs_weight):
    group, nx, ny, nz = probes.shape
    nprobe, nsx, nsy = (lax.axis_size(name) for name in ("probe", "sx", "sy"))
    count = group * nprobe
    deep = ny // 8
    cells = float(nx * nsx * ny * nsy * nz)
    vmem = pl.BlockSpec(memory_space=pltpu.VMEM)
    f32 = jnp.float32
    total = nprobe + nsx + nsy - 3
    return pl.pallas_call(
        functools.partial(kernel, cells),
        out_shape=(
            jax.ShapeDtypeStruct(probes.shape, f32),
            jax.ShapeDtypeStruct((count, count), f32),
        ),
        in_specs=[pl.BlockSpec(memory_space=pl.ANY)] * 4,
        out_specs=(pl.BlockSpec(memory_space=pl.ANY), vmem),
        scratch_shapes=[
            pltpu.VMEM((group, nx + 2, deep, 8, nz), f32),
            pltpu.VMEM((group, nx + 2, deep, 8, nz), f32),
            pltpu.VMEM((nx + 1, deep, 8, nz), f32),
            pltpu.VMEM((2, 7, nx + 2, deep, 8, nz), f32),
            pltpu.VMEM((2, 2, nx, 1, nz), f32),
            pltpu.VMEM((group, nx, nz // LANES, ny, LANES), f32),
            pltpu.VMEM((3, nx, nz // LANES, ny, LANES), f32),
            pltpu.VMEM((nx, nz // LANES, ny, LANES), f32),
            pltpu.VMEM((nx, nz // LANES, ny, LANES), f32),
            pltpu.VMEM((count, nx, deep, 8, nz), f32),
            pltpu.VMEM((2, 2, group, deep, 8, nz), f32),
            pltpu.VMEM((2, group, nx, 1, nz), f32),
            pltpu.VMEM((2, 2, group, nx, 1, nz), f32),
            pltpu.VMEM((nprobe, 8, LANES), f32),
            pltpu.VMEM((nsx, 8, LANES), f32),
            pltpu.VMEM((nsy, 8, LANES), f32),
            pltpu.VMEM((8, LANES), f32),
            pltpu.SemaphoreType.DMA((2,)),
            pltpu.SemaphoreType.DMA((2, 2)),
            pltpu.SemaphoreType.DMA((2,)),
            pltpu.SemaphoreType.DMA((2, 2)),
            pltpu.SemaphoreType.DMA((2, 2)),
            pltpu.SemaphoreType.DMA((2, 2)),
            pltpu.SemaphoreType.DMA((2, 2 * STEPS)),
            pltpu.SemaphoreType.DMA((nprobe, 2 * STEPS)),
            pltpu.SemaphoreType.DMA((total,)),
            pltpu.SemaphoreType.DMA((total,)),
            pltpu.SemaphoreType.DMA((4, 4, nz // LANES)),
            pltpu.SemaphoreType.DMA((4, nz // LANES)),
        ],
        compiler_params=pltpu.CompilerParams(
            collective_id=0, has_side_effects=True, vmem_limit_bytes=60 * 1024 * 1024
        ),
    )(probes, velocity, diffusivity, obs_weight)


def solution(mesh):
    return jax.shard_map(
        shards,
        mesh=mesh,
        in_specs=(
            P("probe", "sx", "sy", None),
            P(None, "sx", "sy", None),
            P("sx", "sy", None),
            P("sx", "sy", None),
        ),
        out_specs=(P("probe", "sx", "sy", None), P()),
        check_vma=False,
    )
```

time: 174 us -> 138 us (0.79)
  Pallas kernels: 168 us -> 133 us
    pallas_call x1, Pallas kernels: 168 us -> 133 us  [shards(): pl.pallas_call(functools.partial(kernel, cells), out_shape=(jax.ShapeDtyp...]
where the time goes in v3:
time: 138 us
  Pallas kernels  133 us (96%)
  local copies, waits for them, and re-layouts  3.76 us (3%)
    pallas_call x1, Pallas kernels, shards(): pl.pallas_call(functools.partial(kernel, cells), out_shape=(jax.ShapeDtyp...  133 us
    unnamed x4, local copies, waits for them, and re-layouts  3.76 us

profile of v3, /device:TPU:1, one launch (start us, length us, event | category | flops | bytes accessed | tf_op | source)
XLA Modules:
  0.0 137.6 jit_solution(5501573491197306090)
XLA Ops:
  0.6 133.2 %shard_map.59 = (f32[2,32,32,256]{3,2,1,0:T(8,128)}, f32[8,8]{1,0:T(8,128)}) custom-call(f32[2,32,32,256]{3,2,1,0:T(8,128)} %probes.1, f32[3,32,32,256]{3,2,1,0:T(8,128)} %velocity.1, f32[32,32,256]{2,1,0:T(8,128)} %diffusivity.1, f32[32,32,256]{2,1,0:T(8,128)} %weight.1), custom_call_target="tpu_custom_call" | custom-call | tf_op jit(solution)/shard_map/pallas_call | solution.py:565
  133.9 0.0 copy-start
  133.9 3.2 %copy.8 = f32[2,32,32,256]{3,2,1,0:T(8,128)} copy(f32[2,32,32,256]{3,2,1,0:T(8,128)} %get-tuple-element.4) | data formatting | bytes 4194304
  137.0 0.0 copy-done
  137.0 0.6 copy.9
Async XLA Ops:
  133.9 3.2 %copy-start = (f32[8,8]{1,0:T(8,128)S(1)}, f32[8,8]{1,0:T(8,128)}, u32[]{:S(2)}) copy-start(f32[8,8]{1,0:T(8,128)} %get-tuple-element.5) | copy-start | bytes 772

commit v4 on v3

--- a/solution.py
+++ b/solution.py
@@ -9,6 +9,7 @@
 
 STEPS = 4
 UNROLL = 1
+ROUTES = (0, 1)
 MESH = pl.DeviceIdType.MESH
 LANES = 128
 C0, PX, MX, PY, MY, PZ, MZ = range(7)
@@ -36,6 +37,7 @@
     got_diffusivity,
     got_weight,
     images,
+    passing,
     x_in,
     y_out,
     y_in,
@@ -51,6 +53,9 @@
     edge_recv,
     image_send,
     image_recv,
+    pass_send,
+    pass_recv,
+    side_send,
     sum_send,
     sum_recv,
     in_sem,
@@ -133,6 +138,13 @@
             peer = lax.rem(at[name] + shift, size[name])
             pl.semaphore_signal(barrier, inc=1, device_id={name: peer}, device_id_type=MESH)
             peers += 1
+
+    across = {
+        "probe": lax.rem(me + size["probe"] // 2, size["probe"]),
+        "sy": at["sy"] + 1 - 2 * lax.rem(at["sy"], 2),
+    }
+    pl.semaphore_signal(barrier, inc=1, device_id=across, device_id_type=MESH)
+    peers += 1
 
     def prepare(x, carry):
         last, first = nz - LANES, 0
@@ -272,64 +284,117 @@
     def fix_y(slot, new, side, mode):
         l, row = (deep - 1, 7) if side else (0, 0)
 
-        def one(x, carry):
-            for t in range(wide):
-                w = tile(t)
-                c = spread(edge[mode, side, x, :, w], (8, LANES))
-                for p in range(group):
-                    add = c * spread(y_in[slot, side, p, x, :, w], (8, LANES))
-                    v = new[p, x + 1, l, :, w] + jnp.where(srow == row, add, 0.0)
-                    new[p, x + 1, l, :, w] = v
-                    y_out[side, p, x, :, w] = v[row : row + 1]
+        many = 4 if nx % 4 == 0 else 1
+
+        def some(n, carry):
+            found = []
+            for k in range(many):
+                x = n * many + k
+                for t in range(wide):
+                    w = tile(t)
+                    c = spread(edge[mode, side, x, :, w], (8, LANES))
+                    for p in range(group):
+                        add = c * spread(y_in[slot, side, p, x, :, w], (8, LANES))
+                        v = new[p, x + 1, l, :, w] + jnp.where(srow == row, add, 0.0)
+                        found.append((p, x, w, v))
+            for p, x, w, v in found:
+                new[p, x + 1, l, :, w] = v
+                y_out[side, p, x, :, w] = v[row : row + 1]
             return carry
 
-        lax.fori_loop(0, nx, one, 0, unroll=4)
+        lax.fori_loop(0, nx // many, some, 0)
 
     chunks = 2 * STEPS
     thick = nx // chunks if nx >= chunks else nx
 
-    def image_copy(pair, target, sem, chunk=None):
-        lead = pl.ds(group * pair, group)
-        if chunk is None:
-            ref, recv, send = images.at[lead], image_recv.at[pair, 0], image_send.at[sem, 0]
-        else:
-            ref = images.at[lead, pl.ds(chunk * thick, thick)]
-            recv, send = image_recv.at[pair, chunk], image_send.at[sem, chunk]
-        return remote(ref, ref, send, recv, "probe", target)
+    def image_copy(pair, target, sem):
+        ref = images.at[pl.ds(group * pair, group)]
+        return remote(
+            ref, ref, image_send.at[sem, 0], image_recv.at[pair, 0, 0], "probe", target
+        )
+
+    def piece(pair, half, chunk):
+        return images.at[group * pair + half, pl.ds(chunk * thick, thick)]
+
+    def straight(half, chunk, came=False):
+        pair = me - 2 if came else me
+        ref = piece(pair, half, chunk)
+        recv = image_recv.at[pair, half, chunk]
+        return remote(ref, ref, image_send.at[1 + half, chunk], recv, "probe", across["probe"])
+
+    def hop(half, chunk, came=False):
+        pair = me - 2 if came else me
+        return pltpu.make_async_remote_copy(
+            src_ref=piece(pair, half, chunk),
+            dst_ref=passing.at[pl.ds(chunk * thick, thick)],
+            send_sem=image_send.at[1 + half, chunk],
+            recv_sem=pass_recv.at[chunk],
+            device_id=across,
+            device_id_type=MESH,
+        )
+
+    def onward(half, chunk):
+        return remote(
+            passing.at[pl.ds(chunk * thick, thick)],
+            piece(me - 2, half, chunk),
+            pass_send.at[chunk],
+            image_recv.at[me - 2, half, chunk],
+            "sy",
+            across["sy"],
+        )
+
+    def beside(half, chunk, pair):
+        ref = piece(pair, half, chunk)
+        send, recv = side_send.at[half, chunk], image_recv.at[pair, half, chunk]
+        return remote(ref, ref, send, recv, "probe", 5 - me)
+
+    def dispatch(chunk):
+        @pl.when(me < 2)
+        def _():
+            for half in range(group):
+                (hop if ROUTES[half] else straight)(half, chunk).start()
+
+    def pass_on(chunk):
+        @pl.when(me >= 2)
+        def _():
+            for half in range(group):
+                if ROUTES[half]:
+                    hop(half, chunk, True).wait_recv()
+                    onward(half, chunk).start()
 
     def relay(chunk):
-        @pl.when(me == 2)
+        @pl.when(me >= 2)
         def _():
-            image_copy(0, 3, 1, chunk).wait_recv()
-            image_copy(0, 3, 1, chunk).start()
-
-        @pl.when(me == 3)
+            for half in range(group):
+                straight(half, chunk, True).wait_recv()
+                beside(half, chunk, me - 2).start()
+
+    def begin(name, side, now, when=True):
+        @pl.when(jnp.logical_and(has[name][side], when))
         def _():
-            image_copy(1, 2, 1, chunk).wait_recv()
-            image_copy(1, 2, 1, chunk).start()
+            face(name, side, now).start()
+
+    def begin_all():
+        for name in ("sy", "sx"):
+            for side in range(2):
+                begin(name, side, 0)
 
     def run(second):
-        def step(i, now, mode):
+        def step(i, now, mode, send):
             old, new = (other_field, field) if now else (field, other_field)
-            for name in ("sy", "sx"):
-                for side in range(2):
-
-                    @pl.when(has[name][side])
-                    def _():
-                        face(name, side, now).start()
-
             if second:
-
-                @pl.when(me < 2)
-                def _():
-                    image_copy(me, me + 2, 1, i).start()
+                dispatch(i)
 
             local(old, new, mode)
             if second:
 
-                @pl.when(i >= 2)
+                @pl.when(i >= 1)
                 def _():
-                    relay(i - 2)
+                    pass_on(i - 1)
+
+                @pl.when(i >= 3)
+                def _():
+                    relay(i - 3)
 
             for name in ("sx", "sy"):
                 for side in range(2):
@@ -340,28 +405,37 @@
                         face(name, side, now, True).wait_recv()
                         (fix_x if name == "sx" else fix_y)(now, new, side, mode)
 
+                    if name == "sy":
+                        begin(name, side, 1 - now, send)
+
+            for side in range(2):
+                begin("sx", side, 1 - now, send)
+
         def both(i, carry):
             mode = 2 * i // STEPS
-            step(2 * i, 0, mode)
-            step(2 * i + 1, 1, mode)
+            step(2 * i, 0, mode, True)
+            step(2 * i + 1, 1, mode, jnp.logical_and(2 * i != STEPS - 2, i != STEPS - 1))
 
             @pl.when(2 * i == STEPS - 2)
             def _():
                 def weigh(x, carry):
+                    found = []
                     for l in range(deep):
                         for t in range(wide):
                             w = tile(t)
                             c = rows_of(got_weight, (x,), l, t)
                             for p in range(group):
-                                v = c * field[p, x + 1, l, :, w]
-                                field[p, x + 1, l, :, w] = v
-                                if l == 0:
-                                    y_out[0, p, x, :, w] = v[0:1]
-                                if l == deep - 1:
-                                    y_out[1, p, x, :, w] = v[7:8]
+                                found.append((p, l, w, c * field[p, x + 1, l, :, w]))
+                    for p, l, w, v in found:
+                        field[p, x + 1, l, :, w] = v
+                        if l == 0:
+                            y_out[0, p, x, :, w] = v[0:1]
+                        if l == deep - 1:
+                            y_out[1, p, x, :, w] = v[7:8]
                     return carry
 
                 lax.fori_loop(0, nx, weigh, 0)
+                begin_all()
                 if not second:
                     for name in ("sx", "sy"):
                         for side in range(2):
@@ -373,6 +447,7 @@
 
             return carry
 
+        begin_all()
         lax.fori_loop(0, STEPS, both, 0)
 
     for name in ("sx", "sy"):
@@ -406,34 +481,40 @@
 
     run(True)
 
-    for chunk in range(chunks - 2, chunks):
+    pass_on(chunks - 1)
+    for chunk in range(chunks - 3, chunks):
         relay(chunk)
 
     @pl.when(me == 0)
     def _():
         image_copy(0, 1, 0).wait_send()
-        for chunk in range(chunks):
-            image_copy(0, 2, 1, chunk).wait_send()
 
     @pl.when(me == 1)
     def _():
-        image_copy(0, 2, 1).wait_recv()
-        for chunk in range(chunks):
-            image_copy(1, 3, 1, chunk).wait_send()
+        image_copy(0, 2, 0).wait_recv()
 
     @pl.when(me == 2)
     def _():
         image_copy(2, 3, 0).wait_send()
-        for chunk in range(chunks):
-            image_copy(0, 3, 1, chunk).wait_send()
-            image_copy(1, 3, 1, chunk).wait_recv()
 
     @pl.when(me == 3)
     def _():
         image_copy(2, 2, 0).wait_recv()
+
+    @pl.when(me < 2)
+    def _():
         for chunk in range(chunks):
-            image_copy(1, 2, 1, chunk).wait_send()
-            image_copy(0, 2, 1, chunk).wait_recv()
+            for half in range(group):
+                (hop if ROUTES[half] else straight)(half, chunk).wait_send()
+
+    @pl.when(me >= 2)
+    def _():
+        for chunk in range(chunks):
+            for half in range(group):
+                if ROUTES[half]:
+                    onward(half, chunk).wait_send()
+                beside(half, chunk, me - 2).wait_send()
+                beside(half, chunk, 3 - me).wait_recv()
 
     trow, tcol = srow, lane
     count = size["probe"] * group
@@ -581,6 +662,7 @@
             pltpu.VMEM((nx, nz // LANES, ny, LANES), f32),
             pltpu.VMEM((nx, nz // LANES, ny, LANES), f32),
             pltpu.VMEM((count, nx, deep, 8, nz), f32),
+            pltpu.VMEM((nx, deep, 8, nz), f32),
             pltpu.VMEM((2, 2, group, deep, 8, nz), f32),
             pltpu.VMEM((2, group, nx, 1, nz), f32),
             pltpu.VMEM((2, 2, group, nx, 1, nz), f32),
@@ -594,8 +676,11 @@
             pltpu.SemaphoreType.DMA((2, 2)),
             pltpu.SemaphoreType.DMA((2, 2)),
             pltpu.SemaphoreType.DMA((2, 2)),
-            pltpu.SemaphoreType.DMA((2, 2 * STEPS)),
-            pltpu.SemaphoreType.DMA((nprobe, 2 * STEPS)),
+            pltpu.SemaphoreType.DMA((1 + group, 2 * STEPS)),
+            pltpu.SemaphoreType.DMA((nprobe, group, 2 * STEPS)),
+            pltpu.SemaphoreType.DMA((2 * STEPS,)),
+            pltpu.SemaphoreType.DMA((2 * STEPS,)),
+            pltpu.SemaphoreType.DMA((group, 2 * STEPS)),
             pltpu.SemaphoreType.DMA((total,)),
             pltpu.SemaphoreType.DMA((total,)),
             pltpu.SemaphoreType.DMA((4, 4, nz // LANES)),

time: 138 us -> 120 us (0.87)
  Pallas kernels: 133 us -> 115 us
    pallas_call x1, Pallas kernels: 133 us -> 115 us  [shards(): pl.pallas_call(functools.partial(kernel, cells), out_shape=(jax.ShapeDtyp...]
where the time goes in v4:
time: 120 us; the launch traced here: 119 us
  Pallas kernels  115 us (96%)
  local copies, waits for them, and re-layouts  3.76 us (3%)
    pallas_call x1, Pallas kernels, shards(): pl.pallas_call(functools.partial(kernel, cells), out_shape=(jax.ShapeDtyp...  115 us
    unnamed x4, local copies, waits for them, and re-layouts  3.76 us

profile of v4, /device:TPU:1, one launch (start us, length us, event | category | flops | bytes accessed | tf_op | source)
XLA Modules:
  0.0 119.3 jit_solution(4268903512599280127)
XLA Ops:
  0.6 114.9 %shard_map.59 = (f32[2,32,32,256]{3,2,1,0:T(8,128)}, f32[8,8]{1,0:T(8,128)}) custom-call(f32[2,32,32,256]{3,2,1,0:T(8,128)} %probes.1, f32[3,32,32,256]{3,2,1,0:T(8,128)} %velocity.1, f32[32,32,256]{2,1,0:T(8,128)} %diffusivity.1, f32[32,32,256]{2,1,0:T(8,128)} %weight.1), custom_call_target="tpu_custom_call" | custom-call | tf_op jit(solution)/shard_map/pallas_call | solution.py:646
  115.5 0.0 copy-start
  115.5 3.2 %copy.8 = f32[2,32,32,256]{3,2,1,0:T(8,128)} copy(f32[2,32,32,256]{3,2,1,0:T(8,128)} %get-tuple-element.4) | data formatting | bytes 4194304
  118.7 0.0 copy-done
  118.7 0.6 copy.9
Async XLA Ops:
  115.5 3.2 %copy-start = (f32[8,8]{1,0:T(8,128)S(1)}, f32[8,8]{1,0:T(8,128)}, u32[]{:S(2)}) copy-start(f32[8,8]{1,0:T(8,128)} %get-tuple-element.5) | copy-start | bytes 772

commit v5 on v4

--- a/solution.py
+++ b/solution.py
@@ -10,6 +10,8 @@
 STEPS = 4
 UNROLL = 1
 ROUTES = (0, 1)
+MANY = 8
+BOTH = 2
 MESH = pl.DeviceIdType.MESH
 LANES = 128
 C0, PX, MX, PY, MY, PZ, MZ = range(7)
@@ -41,9 +43,8 @@
     x_in,
     y_out,
     y_in,
-    sums_probe,
-    sums_sx,
-    sums_sy,
+    sums_slab,
+    sums_line,
     inverse_ref,
     x_send,
     x_recv,
@@ -133,10 +134,20 @@
 
     barrier = pltpu.get_barrier_semaphore()
     peers = 0
-    for name in ("probe", "sx", "sy"):
-        for shift in range(1, size[name]):
-            peer = lax.rem(at[name] + shift, size[name])
-            pl.semaphore_signal(barrier, inc=1, device_id={name: peer}, device_id_type=MESH)
+    nsx = size["sx"]
+    slab, slabs = me * nsx + at["sx"], size["probe"] * nsx
+
+    def in_slab(shift):
+        other = lax.rem(slab + shift, slabs)
+        return {"probe": other // nsx, "sx": lax.rem(other, nsx)}
+
+    def in_line(shift):
+        return {"sy": lax.rem(at["sy"] + shift, size["sy"])}
+
+    stages = ((in_slab, slab, slabs), (in_line, at["sy"], size["sy"]))
+    for who, mine, members in stages:
+        for shift in range(1, members):
+            pl.semaphore_signal(barrier, inc=1, device_id=who(shift), device_id_type=MESH)
             peers += 1
 
     across = {
@@ -208,7 +219,7 @@
                     y_out[1, p, x, :, tile(t)] = field[p, x + 1, deep - 1, 7:8, tile(t)]
             return carry
 
-        lax.fori_loop(0, nx, one, 0)
+        lax.fori_loop(0, nx, one, 0, unroll=4 if nx % 4 == 0 else 1)
 
     fill()
     pl.semaphore_wait(barrier, peers)
@@ -284,7 +295,7 @@
     def fix_y(slot, new, side, mode):
         l, row = (deep - 1, 7) if side else (0, 0)
 
-        many = 4 if nx % 4 == 0 else 1
+        many = MANY if nx % MANY == 0 else 1
 
         def some(n, carry):
             found = []
@@ -383,11 +394,12 @@
         def step(i, now, mode, send):
             old, new = (other_field, field) if now else (field, other_field)
             if second:
+
                 dispatch(i)
 
+
             local(old, new, mode)
-            if second:
-
+            def forward_pieces():
                 @pl.when(i >= 1)
                 def _():
                     pass_on(i - 1)
@@ -396,8 +408,11 @@
                 def _():
                     relay(i - 3)
 
-            for name in ("sx", "sy"):
-                for side in range(2):
+            if second:
+                forward_pieces()
+
+            def receive(name, sides):
+                for side in sides:
 
                     @pl.when(has[name][side])
                     def _():
@@ -408,6 +423,8 @@
                     if name == "sy":
                         begin(name, side, 1 - now, send)
 
+            receive("sx", (0, 1))
+            receive("sy", (0, 1))
             for side in range(2):
                 begin("sx", side, 1 - now, send)
 
@@ -418,15 +435,20 @@
 
             @pl.when(2 * i == STEPS - 2)
             def _():
-                def weigh(x, carry):
+                pair = BOTH if nx % BOTH == 0 else 1
+
+                def weigh(n, carry):
                     found = []
-                    for l in range(deep):
-                        for t in range(wide):
-                            w = tile(t)
-                            c = rows_of(got_weight, (x,), l, t)
-                            for p in range(group):
-                                found.append((p, l, w, c * field[p, x + 1, l, :, w]))
-                    for p, l, w, v in found:
+                    for k in range(pair):
+                        x = n * pair + k
+                        for l in range(deep):
+                            for t in range(wide):
+                                w = tile(t)
+                                c = rows_of(got_weight, (x,), l, t)
+                                for p in range(group):
+                                    v = c * field[p, x + 1, l, :, w]
+                                    found.append((p, x, l, w, v))
+                    for p, x, l, w, v in found:
                         field[p, x + 1, l, :, w] = v
                         if l == 0:
                             y_out[0, p, x, :, w] = v[0:1]
@@ -434,7 +456,7 @@
                             y_out[1, p, x, :, w] = v[7:8]
                     return carry
 
-                lax.fori_loop(0, nx, weigh, 0)
+                lax.fori_loop(0, nx // pair, weigh, 0)
                 begin_all()
                 if not second:
                     for name in ("sx", "sy"):
@@ -468,7 +490,7 @@
             images[group * me + p, x] = field[p, x + 1]
         return carry
 
-    lax.fori_loop(0, nx, keep, 0)
+    lax.fori_loop(0, nx, keep, 0, unroll=2 if nx % 2 == 0 else 1)
 
 
     @pl.when(me == 0)
@@ -549,27 +571,26 @@
     total = lax.fori_loop(0, me + 1, inner, zero)
 
     sem = 0
-    for name, sums in (("probe", sums_probe), ("sx", sums_sx), ("sy", sums_sy)):
-        mine = at[name]
+    for (who, mine, members), sums in zip(stages, (sums_slab, sums_line)):
         sums[mine] = total
 
-        def part(shift, sem):
+        def part(shift):
             return pltpu.make_async_remote_copy(
                 src_ref=sums.at[mine],
                 dst_ref=sums.at[mine],
-                send_sem=sum_send.at[sem],
-                recv_sem=sum_recv.at[sem],
-                device_id={name: lax.rem(mine + shift, size[name])},
+                send_sem=sum_send.at[sem + shift - 1],
+                recv_sem=sum_recv.at[sem + shift - 1],
+                device_id=who(shift),
                 device_id_type=MESH,
             )
 
-        for shift in range(1, size[name]):
-            part(shift, sem + shift - 1).start()
-        for shift in range(1, size[name]):
-            part(shift, sem + shift - 1).wait()
-        sem += size[name] - 1
+        for shift in range(1, members):
+            part(shift).start()
+        for shift in range(1, members):
+            part(shift).wait()
+        sem += members - 1
         total = sums[0]
-        for other in range(1, size[name]):
+        for other in range(1, members):
             total = total + sums[other]
 
     full = (8, LANES)
@@ -642,7 +663,7 @@
     cells = float(nx * nsx * ny * nsy * nz)
     vmem = pl.BlockSpec(memory_space=pltpu.VMEM)
     f32 = jnp.float32
-    total = nprobe + nsx + nsy - 3
+    total = nprobe * nsx + nsy - 2
     return pl.pallas_call(
         functools.partial(kernel, cells),
         out_shape=(
@@ -666,8 +687,7 @@
             pltpu.VMEM((2, 2, group, deep, 8, nz), f32),
             pltpu.VMEM((2, group, nx, 1, nz), f32),
             pltpu.VMEM((2, 2, group, nx, 1, nz), f32),
-            pltpu.VMEM((nprobe, 8, LANES), f32),
-            pltpu.VMEM((nsx, 8, LANES), f32),
+            pltpu.VMEM((nprobe * nsx, 8, LANES), f32),
             pltpu.VMEM((nsy, 8, LANES), f32),
             pltpu.VMEM((8, LANES), f32),
             pltpu.SemaphoreType.DMA((2,)),

time: 120 us -> 118 us (0.983)
    pallas_call x1, Pallas kernels: 115 us -> 114 us  [shards(): pl.pallas_call(functools.partial(kernel, cells), out_shape=(jax.ShapeDtyp...]
where the time goes in v5:
time: 118 us
  Pallas kernels  114 us (97%)
  local copies, waits for them, and re-layouts  3.76 us (3%)
    pallas_call x1, Pallas kernels, shards(): pl.pallas_call(functools.partial(kernel, cells), out_shape=(jax.ShapeDtyp...  114 us
    unnamed x4, local copies, waits for them, and re-layouts  3.76 us

profile of v5, /device:TPU:1, one launch (start us, length us, event | category | flops | bytes accessed | tf_op | source)
XLA Modules:
  0.0 118.0 jit_solution(11517622964586863678)
XLA Ops:
  0.6 113.6 %shard_map.59 = (f32[2,32,32,256]{3,2,1,0:T(8,128)}, f32[8,8]{1,0:T(8,128)}) custom-call(f32[2,32,32,256]{3,2,1,0:T(8,128)} %probes.1, f32[3,32,32,256]{3,2,1,0:T(8,128)} %velocity.1, f32[32,32,256]{2,1,0:T(8,128)} %diffusivity.1, f32[32,32,256]{2,1,0:T(8,128)} %weight.1), custom_call_target="tpu_custom_call" | custom-call | tf_op jit(solution)/shard_map/pallas_call | solution.py:667
  114.3 0.0 copy-start
  114.3 3.2 %copy.8 = f32[2,32,32,256]{3,2,1,0:T(8,128)} copy(f32[2,32,32,256]{3,2,1,0:T(8,128)} %get-tuple-element.4) | data formatting | bytes 4194304
  117.4 0.0 copy-done
  117.4 0.6 copy.9
Async XLA Ops:
  114.3 3.2 %copy-start = (f32[8,8]{1,0:T(8,128)S(1)}, f32[8,8]{1,0:T(8,128)}, u32[]{:S(2)}) copy-start(f32[8,8]{1,0:T(8,128)} %get-tuple-element.5) | copy-start | bytes 772

commit v6 on v5

--- a/solution.py
+++ b/solution.py
@@ -556,7 +556,7 @@
             return tuple(acc)
 
         start = tuple(jnp.zeros((8, nz), jnp.float32) for _ in range(group * group * 2))
-        acc = lax.fori_loop(0, nx, plane, start)
+        acc = lax.fori_loop(0, nx, plane, start, unroll=4 if nx % 4 == 0 else 1)
         for i in range(group):
             for j in range(group):
                 for m in range(2):

time: 118 us -> 118 us (level)
  no operation moved by 1% of the time
where the time goes in v6:
time: 118 us; the launch traced here: 117 us
  Pallas kernels  113 us (96%)
  local copies, waits for them, and re-layouts  3.76 us (3%)
    pallas_call x1, Pallas kernels, shards(): pl.pallas_call(functools.partial(kernel, cells), out_shape=(jax.ShapeDtyp...  113 us
    unnamed x4, local copies, waits for them, and re-layouts  3.76 us

profile of v6, /device:TPU:1, one launch (start us, length us, event | category | flops | bytes accessed | tf_op | source)
XLA Modules:
  0.0 117.5 jit_solution(2401518633091345616)
XLA Ops:
  0.6 113.1 %shard_map.59 = (f32[2,32,32,256]{3,2,1,0:T(8,128)}, f32[8,8]{1,0:T(8,128)}) custom-call(f32[2,32,32,256]{3,2,1,0:T(8,128)} %probes.1, f32[3,32,32,256]{3,2,1,0:T(8,128)} %velocity.1, f32[32,32,256]{2,1,0:T(8,128)} %diffusivity.1, f32[32,32,256]{2,1,0:T(8,128)} %weight.1), custom_call_target="tpu_custom_call" | custom-call | tf_op jit(solution)/shard_map/pallas_call | solution.py:667
  113.7 0.0 copy-start
  113.7 3.2 %copy.8 = f32[2,32,32,256]{3,2,1,0:T(8,128)} copy(f32[2,32,32,256]{3,2,1,0:T(8,128)} %get-tuple-element.4) | data formatting | bytes 4194304
  116.9 0.0 copy-done
  116.9 0.6 copy.9
Async XLA Ops:
  113.7 3.2 %copy-start = (f32[8,8]{1,0:T(8,128)S(1)}, f32[8,8]{1,0:T(8,128)}, u32[]{:S(2)}) copy-start(f32[8,8]{1,0:T(8,128)} %get-tuple-element.5) | copy-start | bytes 772
